TPU v7x, 512 devices: a whole 4x4x16 slice. The times are simulated.
512 devices in a mesh: view: 32 (over y, x, core), tile: 16 (over z).
Axes of the slice: x: 4, y: 4, z: 16, core: 2. Of those that a mesh axis runs over, the one named last changes fastest.
Arguments:
- centers: bfloat16 [384, 2, 128], P('tile'), may hold values from 4 to 28
- log_scales: bfloat16 [384, 2, 128], P('tile'), may hold values from -4 to -1.5
- correlation: bfloat16 [384, 128], P('tile'), may hold values from -0.59765625 to 0.59765625
- opacity_logit: bfloat16 [384, 128], P('tile'), may hold values from -6.5 to -2
- features: bfloat16 [384, 128, 128], P('tile'), may hold values from -16 to 16
- view_offset: float32 [32, 2], P('view'), may hold values from -3 to 3
- block_list: int32 [32, 32, 8], P('view', 'tile'), may hold values from 0 to 383, as said below
- pad_count: int32 [32, 32], P('view', 'tile'), may hold values from 0 to 7, as said below
- block_home: int32 [384], replicated, may hold values from 0 to 383, as said below
- image_grad: bfloat16 [32, 32, 1024, 128], P('view', 'tile'), may hold values from -6 to 6
Outputs:
- image: bfloat16 [32, 32, 1024, 128], P('view', 'tile')
- grad_centers: float32 [384, 2, 128], P('tile')
- grad_log_scales: float32 [384, 2, 128], P('tile')
- grad_correlation: float32 [384, 128], P('tile')
- grad_opacity: float32 [384, 128], P('tile')
- grad_features: float32 [384, 128, 128], P('tile')
Inputs may be any that keep to these rules, and one draw needn't show every extreme that they name: `block_list`: the 2 lists of one view on one index of tile name at most 2 entries whose blocks lie in one shard of 24 rows (through block_home), padded entries included; in every such list set some shard is named exactly 2 times. Padded entries hold valid ids. `pad_count`: the first tile of every view has no padding. `block_home`: A permutation of the block ids.
All inputs are finite; a program needn't handle non-finite values.
Results may differ from a plain program's by a relative error of at most 0.0055.
Values may be sent and summed in bfloat16 or wider, within the bound.
No kernel may reach another device: no remote copies, remote signals or barrier semaphores. Data moves between devices by JAX's collectives and lax.ppermute only.
A program may use at most 64 MiB of HBM per device.

v0:
```python
import jax
import jax.numpy as jnp
from jax import lax
from jax.sharding import PartitionSpec as P

TILE_W = 32


def sent_together(arrays, axis, split_dim, concat_dim, along):
    columns = [a.reshape(*a.shape[:along], -1) for a in arrays]
    both = jnp.concatenate(columns, axis=along)
    result, at, finished = (
        lax.all_to_all(both, axis, split_axis=split_dim, concat_axis=concat_dim, tiled=True),
        0,
        [],
    )
    for a, column in zip(arrays, columns):
        share = result[..., at : at + column.shape[along]]
        finished.append(share.reshape(*share.shape[:along], *a.shape[along:]))
        at += column.shape[along]
    return tuple(finished)


def packed_total(arrays, axis):
    ends = [0]
    for a in arrays:
        ends.append(ends[-1] + a.size)
    running = lax.psum(jnp.concatenate([a.ravel() for a in arrays]), axis)
    return tuple((running[b:e].reshape(a.shape) for a, b, e in zip(arrays, ends, ends[1:])))


def pixel_grid():
    pixel_index = jnp.arange(TILE_W * TILE_W, dtype=jnp.int32)
    across = (pixel_index % TILE_W).astype(jnp.float32) + 0.5
    downward = (pixel_index // TILE_W).astype(jnp.float32) + 0.5
    return (across, downward)


def render_tile(tensors, alive_mask, offset):
    across, downward = pixel_grid()
    feature_width = tensors[4].shape[-1]

    def block_step(running, block_data):
        log_trans, colors = running
        center, log_scale, correl, opacity, feature, alive_flag = block_data
        delta_x = across[:, None] - (center[0] + offset[0])[None, :]
        delta_y = downward[:, None] - (center[1] + offset[1])[None, :]
        coef_a = jnp.exp(log_scale[0])
        coef_c = jnp.exp(log_scale[1])
        coef_b = correl * jnp.sqrt(coef_a * coef_c)
        quadric = (
            coef_a[None, :] * delta_x * delta_x
            + 2.0 * coef_b[None, :] * delta_x * delta_y
            + coef_c[None, :] * delta_y * delta_y
        )
        alphas = jax.nn.sigmoid(opacity)[None, :] * jnp.exp(-0.5 * quadric) * alive_flag
        log_keep = jnp.log1p(-alphas)
        before = jnp.cumsum(log_keep, axis=1) - log_keep
        weight = (alphas * jnp.exp(log_trans[:, None] + before)).astype(jnp.bfloat16)
        colors = colors + jnp.dot(
            weight, feature.astype(jnp.bfloat16), preferred_element_type=jnp.float32
        )
        log_trans = log_trans + jnp.sum(log_keep, axis=1)
        return ((log_trans, colors), None)

    start_state = (
        jnp.zeros((across.shape[0],), jnp.float32),
        jnp.zeros((across.shape[0], feature_width), jnp.float32),
    )
    (log_trans, colors), unused = lax.scan(
        jax.checkpoint(block_step), start_state, tuple(tensors) + (alive_mask,)
    )
    return colors


def shards(
    centers,
    log_scales,
    correlation,
    opacity_logit,
    features,
    view_offset,
    block_list,
    pad_count,
    block_home,
    image_grad,
):
    tile_count = lax.axis_size("tile")
    shard_blocks = centers.shape[0]
    tiles_here = block_list.shape[1]
    list_length = block_list.shape[2]
    slot_count = tiles_here * list_length
    capacity = (slot_count + tile_count - 1) // tile_count + 1
    buffer_size = tile_count * capacity
    block_ids = block_list.reshape(slot_count)
    storage = jnp.take(block_home, block_ids)
    owner_of = storage // shard_blocks
    local_slot = storage % shard_blocks
    owner_hits = (owner_of[:, None] == jnp.arange(tile_count, dtype=jnp.int32)[None, :]).astype(
        jnp.int32
    )
    earlier = jnp.cumsum(owner_hits, axis=0) - owner_hits
    owner_rank = jnp.sum(earlier * owner_hits, axis=1)
    position = owner_of * capacity + owner_rank
    placing = position[:, None] == jnp.arange(buffer_size, dtype=jnp.int32)[None, :]
    requests = jnp.sum(jnp.where(placing, local_slot[:, None] + 1, 0), axis=0) - 1
    asked_slots = lax.all_to_all(requests, "tile", split_axis=0, concat_axis=0, tiled=True)
    params = (centers, log_scales, correlation, opacity_logit, features)
    chosen = jnp.clip(asked_slots, 0, shard_blocks - 1)
    outgoing = tuple((jnp.take(array_in, chosen, axis=0) for array_in in params))
    arrived = sent_together(
        (outgoing[0], outgoing[1], outgoing[2], outgoing[3], outgoing[4]), "tile", 0, 0, 1
    )
    picked = tuple((jnp.take(array_in, position, axis=0) for array_in in arrived))
    offset = view_offset[0]
    images = []
    slot_grads = []
    for tile_number in range(tiles_here):
        first_row = tile_number * list_length
        inputs = tuple(
            (
                array_in[first_row : first_row + list_length].astype(jnp.float32)
                for array_in in picked
            )
        )
        alive_mask = (
            jnp.arange(list_length, dtype=jnp.int32) < list_length - pad_count[0, tile_number]
        ).astype(jnp.float32)
        colors, pullback = jax.vjp(
            lambda *tensors: render_tile(tensors, alive_mask, offset), *inputs
        )
        images.append(colors.astype(jnp.bfloat16))
        slot_grads.append(
            tuple((grad_in for grad_in in pullback(image_grad[0, tile_number].astype(jnp.float32))))
        )
    image_out = jnp.stack(images)[None]
    joined_grads = tuple(
        (
            jnp.concatenate([grad_set[member] for grad_set in slot_grads], axis=0)
            for member in range(5)
        )
    )
    placing_float = placing.astype(jnp.float32)
    outbound = tuple(
        (
            jnp.tensordot(placing_float, grad_in, axes=(0, 0), precision=lax.Precision.HIGHEST)
            for grad_in in joined_grads
        )
    )
    returned = sent_together(
        (outbound[0], outbound[1], outbound[2], outbound[3], outbound[4]), "tile", 0, 0, 1
    )
    picking = (asked_slots[:, None] == jnp.arange(shard_blocks, dtype=jnp.int32)[None, :]).astype(
        jnp.float32
    )
    shard_grads = tuple(
        (
            jnp.tensordot(picking, grad_in, axes=(0, 0), precision=lax.Precision.HIGHEST)
            for grad_in in returned
        )
    )
    totals = packed_total(
        (shard_grads[0], shard_grads[1], shard_grads[2], shard_grads[3], shard_grads[4]), "view"
    )
    return (image_out, totals[0], totals[1], totals[2], totals[3], totals[4])


def solution(mesh):
    in_specs = (
        P("tile", None, None),
        P("tile", None, None),
        P("tile", None),
        P("tile", None),
        P("tile", None, None),
        P("view", None),
        P("view", "tile", None),
        P("view", "tile"),
        P(),
        P("view", "tile", None, None),
    )
    out_specs = (
        P("view", "tile", None, None),
        P("tile", None, None),
        P("tile", None, None),
        P("tile", None),
        P("tile", None),
        P("tile", None, None),
    )
    return jax.shard_map(shards, mesh=mesh, in_specs=in_specs, out_specs=out_specs, check_vma=False)
```

profile of v0, /device:TPU:1, one launch (start us, length us, event | category | flops | bytes accessed | tf_op | source)
XLA Modules:
  0.0 967.6 jit_solution(10539308265335564460)
XLA Ops:
  10.7 26.9 %all_to_all.27 = s32[16,2,1]{1,2,0:T(1,128)S(1)} all-to-all(s32[16,2,1]{1,2,0:T(1,128)S(1)} %bitcast.443), channel_id=1, replica_groups=mesh['view'=32,'tile'=16] {'tile'}, dimensions={0} | all-to-all | bytes 256 | tf_op jit(solution)/shard_map/all_to_all | solution.py:107
  48.6 2.2 fusion.151
  50.8 3.8 all-to-all-start.1
  58.7 43.1 %all-to-all-done.1 = bf16[16,2,17152]{2,1,0:T(2,128)(2,1)S(1)} async-done(((bf16[16,2,17152]{2,1,0:T(2,128)(2,1)}), bf16[16,2,17152]{2,1,0:T(2,128)(2,1)S(1)}, u32[]{:S(2)}, u32[]{:S(2)}) %all-to-all-start.1) | async-done | bytes 1097760 | tf_op jit(solution)/shard_map/all_to_all | solution.py:13
  106.5 47.7 %while.85 = (s32[]{:T(128)}, f32[1024]{0:T(1024)S(1)}, f32[1024,128]{1,0:T(8,128)}, f32[8,1024]{1,0:T(8,128)S(1)}, f32[8,128]{1,0:T(8,128)S(1)}, /*index=5*/f32[...) while((s32[]{:T(128)}, f32[1024]{0:T(1024)S(1)}, ...), condition=%wide.region_10.15_spmd.clone, body=%wide.region_7.14_spmd.clone.sunk | while | flops 54808576 | bytes 7447820 | solution.py:70
  154.9 53.0 %while.84 = (s32[]{:T(128)}, f32[1024]{0:T(1024)S(1)}, f32[1024,128]{1,0:T(8,128)S(1)}, f32[8,1024]{1,0:T(8,128)S(1)}, f32[8,128]{1,0:T(8,128)}, /*index=5*/f32[...) while((s32[]{:T(128)}, f32[1024]{0:T(1024)S(1)}, ...), condition=%wide.region_6.11_spmd.clone, body=%wide.region_3.10_spmd.clone.sunk | while | flops 54808576 | bytes 3253460 | solution.py:70
  211.3 246.4 %while.87 = (s32[]{:T(128)}, f32[1024]{0:T(1024)S(1)}, bf16[1024,128]{1,0:T(8,128)(2,1)S(1)}, f32[8,2,128]{2,0,1:T(8,128)}, f32[8,2,128]{2,0,1:T(8,128)}, /*inde...) while((s32[]{:T(128)}, f32[1024]{0:T(1024)S(1)}, ...), condition=%wide.region_32.37_spmd.clone, body=%wide.region_22.36_spmd.clone.sunk | while | flops 113807872 | bytes 15444131 | solution.py:70
  219.2 8.8 reduce_window_sum.100
  228.2 2.0 fusion.296
  235.7 2.4 fusion.298
  238.1 2.9 dynamic_update_slice.135
  248.8 8.8 reduce_window_sum.100
  257.8 2.0 fusion.296
  265.2 2.4 fusion.298
  267.6 2.9 dynamic_update_slice.135
  278.3 8.8 reduce_window_sum.100
  287.3 2.0 fusion.296
  294.7 2.4 fusion.298
  297.1 2.9 dynamic_update_slice.135
  307.8 8.8 reduce_window_sum.100
  316.8 2.0 fusion.296
  324.3 2.4 fusion.298
  326.7 2.9 dynamic_update_slice.135
  337.3 8.8 reduce_window_sum.100
  346.3 2.0 fusion.296
  353.8 2.4 fusion.298
  356.2 2.9 dynamic_update_slice.135
  366.8 8.8 reduce_window_sum.100
  375.8 2.0 fusion.296
  383.3 2.4 fusion.298
  385.7 2.9 dynamic_update_slice.135
  396.4 8.8 reduce_window_sum.100
  405.4 2.0 fusion.296
  412.8 2.4 fusion.298
  415.2 2.9 dynamic_update_slice.135
  425.9 8.8 reduce_window_sum.100
  434.9 2.0 fusion.296
  442.4 2.4 fusion.298
  444.7 2.9 dynamic_update_slice.135
  460.3 226.0 %while.86 = (s32[]{:T(128)}, f32[1024]{0:T(1024)S(1)}, bf16[1024,128]{1,0:T(8,128)(2,1)}, f32[8,2,128]{2,0,1:T(8,128)S(1)}, f32[8,2,128]{2,0,1:T(8,128)}, /*inde...) while((s32[]{:T(128)}, f32[1024]{0:T(1024)S(1)}, ...), condition=%wide.region_21.26_spmd.clone, body=%wide.region_11.25_spmd.clone.sunk | while | flops 113807872 | bytes 14067563 | solution.py:70
  469.1 8.8 reduce_window_sum.98
  478.2 2.0 fusion.284
  485.6 2.9 dynamic_update_slice.130
  497.4 8.8 reduce_window_sum.98
  513.8 2.9 dynamic_update_slice.130
  525.6 8.8 reduce_window_sum.98
  542.0 2.9 dynamic_update_slice.130
  553.8 8.8 reduce_window_sum.98
  570.3 2.9 dynamic_update_slice.130
  582.0 8.8 reduce_window_sum.98
  598.5 2.9 dynamic_update_slice.130
  610.3 8.8 reduce_window_sum.98
  626.7 2.9 dynamic_update_slice.130
  638.5 8.8 reduce_window_sum.98
  655.0 2.9 dynamic_update_slice.130
  666.7 8.8 reduce_window_sum.98
  683.2 2.9 dynamic_update_slice.130
  688.9 2.3 fusion.152
  691.3 2.5 copy.76
  693.8 2.5 concatenate.58
  700.3 114.1 %all_to_all.28 = f32[16,2,17152]{2,1,0:T(2,128)} all-to-all(f32[16,2,17152]{2,1,0:T(2,128)} %constant_dynamic-update-slice_fusion.4), channel_id=1, replica_groups=mesh['view'=32,'tile'=16] {'tile'}, dimensions={0} | all-to-all | bytes 4390912 | tf_op jit(solution)/shard_map/all_to_all | solution.py:13
  814.4 2.8 all_to_all.23
  824.7 130.5 %all-reduce.10.cloned.1.call-done = f32[411648]{0:T(1024)} async-done(((f32[411648]{0:T(1024)}), f32[411648]{0:T(1024)}) %all-reduce.10.cloned.1.call-update) | async-done | bytes 1646608 | tf_op jit(solution)/shard_map/psum | solution.py:28
  957.9 2.7 slice.378
  (1097 shorter events, 378.1 us)
Async XLA Ops:
  7.2 38.3 %copy-start = (bf16[24,128,128]{2,1,0:T(8,128)(2,1)S(1)}, bf16[24,128,128]{2,1,0:T(8,128)(2,1)}, u32[]{:S(2)}) copy-start(bf16[24,128,128]{2,1,0:T(8,128)(2,1)} %param.30) | copy-start | bytes 2359300
  10.5 47.3 %copy-start.34 = (s32[16]{0:T(128)}, s32[16]{0:T(128)S(1)}, u32[]{:S(2)}) copy-start(s32[16]{0:T(128)S(1)} %get-tuple-element.1271) | copy-start | bytes 196
  48.6 6.1 copy-start.33
  48.6 8.6 copy-start.14
  50.8 7.0 copy-start.9
  50.8 51.0 %all-to-all-start.1 = ((bf16[16,2,17152]{2,1,0:T(2,128)(2,1)}), bf16[16,2,17152]{2,1,0:T(2,128)(2,1)S(1)}, u32[]{:S(2)}, u32[]{:S(2)}) async-start(bf16[16,2,17152]{2,1,0:T(2,128)(2,1)} %fusion.151), calls=%async_computation.1 | async-start | bytes 2195456 | tf_op jit(solution)/shard_map/all_to_all | solution.py:13
  54.6 900.6 %all-reduce.10.cloned.1.call-start = ((), (), s32[]{:S(2)}) async-start(), calls=%async_computation.3 | async-start | bytes 3293184 | tf_op jit(solution)/shard_map/psum | solution.py:28
  154.8 56.4 %copy-start.12 = (bf16[1024,128]{1,0:T(8,128)(2,1)S(1)}, bf16[1024,128]{1,0:T(8,128)(2,1)}, u32[]{:S(2)}) copy-start(bf16[1024,128]{1,0:T(8,128)(2,1)} %get-tuple-element.1969) | copy-start | bytes 786436
  154.9 56.4 %copy-start.37 = (f32[8]{0:T(128)S(1)}, f32[8]{0:T(128)}, u32[]{:S(2)}) copy-start(f32[8]{0:T(128)} %copy-done.36) | copy-start | bytes 100
  211.6 6.1 copy-start.15
  211.6 6.1 copy-start.19
  230.3 10.7 %copy-start.3 = (bf16[8,128,128]{2,1,0:T(8,128)(2,1)S(1)}, bf16[8,128,128]{2,1,0:T(8,128)(2,1)}, u32[]{:S(2)}) copy-start(bf16[8,128,128]{2,1,0:T(8,128)(2,1)} %copy-done.2) | copy-start | bytes 786436 | tf_op jit(solution)/shard_map/transpose(jvp())/while
  230.3 10.7 %copy-start.13 = (bf16[1024,128]{1,0:T(8,128)(2,1)S(1)}, bf16[1024,128]{1,0:T(8,128)(2,1)}, u32[]{:S(2)}) copy-start(bf16[1024,128]{1,0:T(8,128)(2,1)} %get-tuple-element.2114) | copy-start | bytes 786436 | tf_op jit(solution)/shard_map/transpose(jvp())/while
  230.3 10.7 %copy-start.16 = (f32[8,1024]{1,0:T(8,128)S(1)}, f32[8,1024]{1,0:T(8,128)}, u32[]{:S(2)}) copy-start(f32[8,1024]{1,0:T(8,128)} %copy-done.15) | copy-start | bytes 98308 | tf_op jit(solution)/shard_map/transpose(jvp())/while
  230.3 10.7 %copy-start.20 = (f32[8,2,128]{2,1,0:T(2,128)S(1)}, f32[8,2,128]{2,1,0:T(2,128)}, u32[]{:S(2)}) copy-start(f32[8,2,128]{2,1,0:T(2,128)} %copy-done.19) | copy-start | bytes 24580 | tf_op jit(solution)/shard_map/transpose(jvp())/while
  230.3 10.7 %copy-start.38 = (f32[8]{0:T(128)S(1)}, f32[8]{0:T(128)}, u32[]{:S(2)}) copy-start(f32[8]{0:T(128)} %get-tuple-element.2146) | copy-start | bytes 100 | tf_op jit(solution)/shard_map/transpose(jvp())/while
  241.1 6.1 copy-start.15
  241.1 6.1 copy-start.19
  259.8 10.7 %copy-start.3 = (bf16[8,128,128]{2,1,0:T(8,128)(2,1)S(1)}, bf16[8,128,128]{2,1,0:T(8,128)(2,1)}, u32[]{:S(2)}) copy-start(bf16[8,128,128]{2,1,0:T(8,128)(2,1)} %copy-done.2) | copy-start | bytes 786436 | tf_op jit(solution)/shard_map/transpose(jvp())/while
  259.8 10.7 %copy-start.13 = (bf16[1024,128]{1,0:T(8,128)(2,1)S(1)}, bf16[1024,128]{1,0:T(8,128)(2,1)}, u32[]{:S(2)}) copy-start(bf16[1024,128]{1,0:T(8,128)(2,1)} %get-tuple-element.2114) | copy-start | bytes 786436 | tf_op jit(solution)/shard_map/transpose(jvp())/while
  259.8 10.7 %copy-start.16 = (f32[8,1024]{1,0:T(8,128)S(1)}, f32[8,1024]{1,0:T(8,128)}, u32[]{:S(2)}) copy-start(f32[8,1024]{1,0:T(8,128)} %copy-done.15) | copy-start | bytes 98308 | tf_op jit(solution)/shard_map/transpose(jvp())/while
  259.8 10.7 %copy-start.20 = (f32[8,2,128]{2,1,0:T(2,128)S(1)}, f32[8,2,128]{2,1,0:T(2,128)}, u32[]{:S(2)}) copy-start(f32[8,2,128]{2,1,0:T(2,128)} %copy-done.19) | copy-start | bytes 24580 | tf_op jit(solution)/shard_map/transpose(jvp())/while
  259.8 10.7 %copy-start.38 = (f32[8]{0:T(128)S(1)}, f32[8]{0:T(128)}, u32[]{:S(2)}) copy-start(f32[8]{0:T(128)} %get-tuple-element.2146) | copy-start | bytes 100 | tf_op jit(solution)/shard_map/transpose(jvp())/while
  270.6 6.1 copy-start.15
  270.6 6.1 copy-start.19
  289.3 10.7 %copy-start.3 = (bf16[8,128,128]{2,1,0:T(8,128)(2,1)S(1)}, bf16[8,128,128]{2,1,0:T(8,128)(2,1)}, u32[]{:S(2)}) copy-start(bf16[8,128,128]{2,1,0:T(8,128)(2,1)} %copy-done.2) | copy-start | bytes 786436 | tf_op jit(solution)/shard_map/transpose(jvp())/while
  289.3 10.7 %copy-start.13 = (bf16[1024,128]{1,0:T(8,128)(2,1)S(1)}, bf16[1024,128]{1,0:T(8,128)(2,1)}, u32[]{:S(2)}) copy-start(bf16[1024,128]{1,0:T(8,128)(2,1)} %get-tuple-element.2114) | copy-start | bytes 786436 | tf_op jit(solution)/shard_map/transpose(jvp())/while
  289.3 10.7 %copy-start.16 = (f32[8,1024]{1,0:T(8,128)S(1)}, f32[8,1024]{1,0:T(8,128)}, u32[]{:S(2)}) copy-start(f32[8,1024]{1,0:T(8,128)} %copy-done.15) | copy-start | bytes 98308 | tf_op jit(solution)/shard_map/transpose(jvp())/while
  289.3 10.7 %copy-start.20 = (f32[8,2,128]{2,1,0:T(2,128)S(1)}, f32[8,2,128]{2,1,0:T(2,128)}, u32[]{:S(2)}) copy-start(f32[8,2,128]{2,1,0:T(2,128)} %copy-done.19) | copy-start | bytes 24580 | tf_op jit(solution)/shard_map/transpose(jvp())/while
  289.4 10.7 %copy-start.38 = (f32[8]{0:T(128)S(1)}, f32[8]{0:T(128)}, u32[]{:S(2)}) copy-start(f32[8]{0:T(128)} %get-tuple-element.2146) | copy-start | bytes 100 | tf_op jit(solution)/shard_map/transpose(jvp())/while
  300.1 6.1 copy-start.15
  300.1 6.1 copy-start.19
  318.8 10.7 %copy-start.3 = (bf16[8,128,128]{2,1,0:T(8,128)(2,1)S(1)}, bf16[8,128,128]{2,1,0:T(8,128)(2,1)}, u32[]{:S(2)}) copy-start(bf16[8,128,128]{2,1,0:T(8,128)(2,1)} %copy-done.2) | copy-start | bytes 786436 | tf_op jit(solution)/shard_map/transpose(jvp())/while
  318.8 10.7 %copy-start.13 = (bf16[1024,128]{1,0:T(8,128)(2,1)S(1)}, bf16[1024,128]{1,0:T(8,128)(2,1)}, u32[]{:S(2)}) copy-start(bf16[1024,128]{1,0:T(8,128)(2,1)} %get-tuple-element.2114) | copy-start | bytes 786436 | tf_op jit(solution)/shard_map/transpose(jvp())/while
  318.9 10.7 %copy-start.16 = (f32[8,1024]{1,0:T(8,128)S(1)}, f32[8,1024]{1,0:T(8,128)}, u32[]{:S(2)}) copy-start(f32[8,1024]{1,0:T(8,128)} %copy-done.15) | copy-start | bytes 98308 | tf_op jit(solution)/shard_map/transpose(jvp())/while
  318.9 10.7 %copy-start.20 = (f32[8,2,128]{2,1,0:T(2,128)S(1)}, f32[8,2,128]{2,1,0:T(2,128)}, u32[]{:S(2)}) copy-start(f32[8,2,128]{2,1,0:T(2,128)} %copy-done.19) | copy-start | bytes 24580 | tf_op jit(solution)/shard_map/transpose(jvp())/while
  318.9 10.7 %copy-start.38 = (f32[8]{0:T(128)S(1)}, f32[8]{0:T(128)}, u32[]{:S(2)}) copy-start(f32[8]{0:T(128)} %get-tuple-element.2146) | copy-start | bytes 100 | tf_op jit(solution)/shard_map/transpose(jvp())/while
  329.6 6.1 copy-start.15
  329.6 6.1 copy-start.19
  348.4 10.7 %copy-start.3 = (bf16[8,128,128]{2,1,0:T(8,128)(2,1)S(1)}, bf16[8,128,128]{2,1,0:T(8,128)(2,1)}, u32[]{:S(2)}) copy-start(bf16[8,128,128]{2,1,0:T(8,128)(2,1)} %copy-done.2) | copy-start | bytes 786436 | tf_op jit(solution)/shard_map/transpose(jvp())/while
  348.4 10.7 %copy-start.13 = (bf16[1024,128]{1,0:T(8,128)(2,1)S(1)}, bf16[1024,128]{1,0:T(8,128)(2,1)}, u32[]{:S(2)}) copy-start(bf16[1024,128]{1,0:T(8,128)(2,1)} %get-tuple-element.2114) | copy-start | bytes 786436 | tf_op jit(solution)/shard_map/transpose(jvp())/while
  348.4 10.7 %copy-start.16 = (f32[8,1024]{1,0:T(8,128)S(1)}, f32[8,1024]{1,0:T(8,128)}, u32[]{:S(2)}) copy-start(f32[8,1024]{1,0:T(8,128)} %copy-done.15) | copy-start | bytes 98308 | tf_op jit(solution)/shard_map/transpose(jvp())/while
  348.4 10.7 %copy-start.20 = (f32[8,2,128]{2,1,0:T(2,128)S(1)}, f32[8,2,128]{2,1,0:T(2,128)}, u32[]{:S(2)}) copy-start(f32[8,2,128]{2,1,0:T(2,128)} %copy-done.19) | copy-start | bytes 24580 | tf_op jit(solution)/shard_map/transpose(jvp())/while
  348.4 10.7 %copy-start.38 = (f32[8]{0:T(128)S(1)}, f32[8]{0:T(128)}, u32[]{:S(2)}) copy-start(f32[8]{0:T(128)} %get-tuple-element.2146) | copy-start | bytes 100 | tf_op jit(solution)/shard_map/transpose(jvp())/while
  359.2 6.1 copy-start.15
  359.2 6.1 copy-start.19
  377.9 10.7 %copy-start.3 = (bf16[8,128,128]{2,1,0:T(8,128)(2,1)S(1)}, bf16[8,128,128]{2,1,0:T(8,128)(2,1)}, u32[]{:S(2)}) copy-start(bf16[8,128,128]{2,1,0:T(8,128)(2,1)} %copy-done.2) | copy-start | bytes 786436 | tf_op jit(solution)/shard_map/transpose(jvp())/while
  377.9 10.7 %copy-start.13 = (bf16[1024,128]{1,0:T(8,128)(2,1)S(1)}, bf16[1024,128]{1,0:T(8,128)(2,1)}, u32[]{:S(2)}) copy-start(bf16[1024,128]{1,0:T(8,128)(2,1)} %get-tuple-element.2114) | copy-start | bytes 786436 | tf_op jit(solution)/shard_map/transpose(jvp())/while
  377.9 10.7 %copy-start.16 = (f32[8,1024]{1,0:T(8,128)S(1)}, f32[8,1024]{1,0:T(8,128)}, u32[]{:S(2)}) copy-start(f32[8,1024]{1,0:T(8,128)} %copy-done.15) | copy-start | bytes 98308 | tf_op jit(solution)/shard_map/transpose(jvp())/while
  377.9 10.7 %copy-start.20 = (f32[8,2,128]{2,1,0:T(2,128)S(1)}, f32[8,2,128]{2,1,0:T(2,128)}, u32[]{:S(2)}) copy-start(f32[8,2,128]{2,1,0:T(2,128)} %copy-done.19) | copy-start | bytes 24580 | tf_op jit(solution)/shard_map/transpose(jvp())/while
  377.9 10.7 %copy-start.38 = (f32[8]{0:T(128)S(1)}, f32[8]{0:T(128)}, u32[]{:S(2)}) copy-start(f32[8]{0:T(128)} %get-tuple-element.2146) | copy-start | bytes 100 | tf_op jit(solution)/shard_map/transpose(jvp())/while
  388.7 6.1 copy-start.15
  407.4 10.7 %copy-start.3 = (bf16[8,128,128]{2,1,0:T(8,128)(2,1)S(1)}, bf16[8,128,128]{2,1,0:T(8,128)(2,1)}, u32[]{:S(2)}) copy-start(bf16[8,128,128]{2,1,0:T(8,128)(2,1)} %copy-done.2) | copy-start | bytes 786436 | tf_op jit(solution)/shard_map/transpose(jvp())/while
  407.4 10.7 %copy-start.13 = (bf16[1024,128]{1,0:T(8,128)(2,1)S(1)}, bf16[1024,128]{1,0:T(8,128)(2,1)}, u32[]{:S(2)}) copy-start(bf16[1024,128]{1,0:T(8,128)(2,1)} %get-tuple-element.2114) | copy-start | bytes 786436 | tf_op jit(solution)/shard_map/transpose(jvp())/while
  407.4 10.7 %copy-start.16 = (f32[8,1024]{1,0:T(8,128)S(1)}, f32[8,1024]{1,0:T(8,128)}, u32[]{:S(2)}) copy-start(f32[8,1024]{1,0:T(8,128)} %copy-done.15) | copy-start | bytes 98308 | tf_op jit(solution)/shard_map/transpose(jvp())/while
  407.4 10.7 %copy-start.20 = (f32[8,2,128]{2,1,0:T(2,128)S(1)}, f32[8,2,128]{2,1,0:T(2,128)}, u32[]{:S(2)}) copy-start(f32[8,2,128]{2,1,0:T(2,128)} %copy-done.19) | copy-start | bytes 24580 | tf_op jit(solution)/shard_map/transpose(jvp())/while
  407.4 10.7 %copy-start.38 = (f32[8]{0:T(128)S(1)}, f32[8]{0:T(128)}, u32[]{:S(2)}) copy-start(f32[8]{0:T(128)} %get-tuple-element.2146) | copy-start | bytes 100 | tf_op jit(solution)/shard_map/transpose(jvp())/while
  436.9 10.7 %copy-start.3 = (bf16[8,128,128]{2,1,0:T(8,128)(2,1)S(1)}, bf16[8,128,128]{2,1,0:T(8,128)(2,1)}, u32[]{:S(2)}) copy-start(bf16[8,128,128]{2,1,0:T(8,128)(2,1)} %copy-done.2) | copy-start | bytes 786436 | tf_op jit(solution)/shard_map/transpose(jvp())/while
  436.9 10.7 %copy-start.13 = (bf16[1024,128]{1,0:T(8,128)(2,1)S(1)}, bf16[1024,128]{1,0:T(8,128)(2,1)}, u32[]{:S(2)}) copy-start(bf16[1024,128]{1,0:T(8,128)(2,1)} %get-tuple-element.2114) | copy-start | bytes 786436 | tf_op jit(solution)/shard_map/transpose(jvp())/while
  436.9 10.7 %copy-start.16 = (f32[8,1024]{1,0:T(8,128)S(1)}, f32[8,1024]{1,0:T(8,128)}, u32[]{:S(2)}) copy-start(f32[8,1024]{1,0:T(8,128)} %copy-done.15) | copy-start | bytes 98308 | tf_op jit(solution)/shard_map/transpose(jvp())/while
  437.0 10.7 %copy-start.20 = (f32[8,2,128]{2,1,0:T(2,128)S(1)}, f32[8,2,128]{2,1,0:T(2,128)}, u32[]{:S(2)}) copy-start(f32[8,2,128]{2,1,0:T(2,128)} %copy-done.19) | copy-start | bytes 24580 | tf_op jit(solution)/shard_map/transpose(jvp())/while
  437.0 10.7 %copy-start.38 = (f32[8]{0:T(128)S(1)}, f32[8]{0:T(128)}, u32[]{:S(2)}) copy-start(f32[8]{0:T(128)} %get-tuple-element.2146) | copy-start | bytes 100 | tf_op jit(solution)/shard_map/transpose(jvp())/while
  460.3 226.0 %copy-start.27 = (f32[8,2,128]{2,0,1:T(8,128)S(1)}, f32[8,2,128]{2,0,1:T(8,128)}, u32[]{:S(2)}) copy-start(f32[8,2,128]{2,0,1:T(8,128)} %get-tuple-element.2128) | copy-start | bytes 24580
  460.3 227.6 %copy-start.28 = (f32[8,2,128]{2,0,1:T(8,128)S(1)}, f32[8,2,128]{2,0,1:T(8,128)}, u32[]{:S(2)}) copy-start(f32[8,2,128]{2,0,1:T(8,128)} %get-tuple-element.2129) | copy-start | bytes 24580
  (61 other events, 194.5 us)
Sparse Core Ops, SparseCore 0:
  822.9 132.2 all-reduce.9
where the time goes:
time: 976 us; the launch traced here: 968 us
  other arithmetic  280 us (29%)
  local copies, waits for them, and re-layouts  256 us (26%)
  waiting for transfers between devices  174 us (18%)
  blocking collectives  141 us (14%)
  matrix products  82.2 us (8%)
  between operations  16.2 us (2%)
  loops' own time  14.9 us (2%)
    another operation x48, other arithmetic, block_step(): before = jnp.cumsum(log_keep, axis=1) - log_keep  157 us
    psum x1, waiting for transfers between devices, packed_total(): running = lax.psum(jnp.concatenate([a.ravel() for a in arrays]), axis)  130 us
    dynamic_update_slice x96, local copies, waits for them, and re-layouts, render_tile(): lax.scan(jax.checkpoint(block_step), start_state, tuple(tensors) + (alive...  122 us
    all_to_all x1, blocking collectives, sent_together(): lax.all_to_all(both, axis, split_axis=split_dim, concat_axis=concat_dim,...  114 us
    dot_general x48, matrix products, block_step(): jnp.dot(weight, feature.astype(jnp.bfloat16), preferred_element_type=jnp....  74.8 us
    all_to_all x1, waiting for transfers between devices, sent_together(): lax.all_to_all(both, axis, split_axis=split_dim, concat_axis=concat_dim,...  43.1 us
    log1p x32, other arithmetic, block_step(): log_keep = jnp.log1p(-alphas)  36.5 us
    reduce_sum x16, other arithmetic, block_step(): coef_c[None, :] * delta_y * delta_y  32.2 us
  transfers between devices with their start and end apart: 2, of which 2 were waited for; matrix products, arithmetic and copies ran while one was open for 0% of the time, Pallas kernels for 0%

commit v1 on v0

v1 whole, which is shorter than its diff:
```python
import functools

import jax
import jax.numpy as jnp
from jax import lax
from jax.experimental import pallas as pl
from jax.experimental.pallas import tpu as pltpu
from jax.sharding import PartitionSpec as P

TILE_W = 32
PIX = 1024
F = 128
BLOCK = 128
LIST = 8
LANES = 128
WIDTH = 640
PARAMS = 8
LOG2E = 1.4426950408889634
CHUNKS = PIX // LANES
f32 = jnp.float32
bf16 = jnp.bfloat16

NN = (((1,), (0,)), ((), ()))
NT = (((1,), (1,)), ((), ()))
TN = (((0,), (0,)), ((), ()))


def dot(a, b, dims=NN, precision=None):
    return lax.dot_general(a, b, dims, precision=precision, preferred_element_type=f32)


def iota(shape, dim):
    return lax.broadcasted_iota(jnp.int32, shape, dim)


def lane_roll(x, shift):
    return pltpu.roll(x, shift % LANES, 1)


def split_pairs(x):
    kept = jnp.where(iota(x.shape, 1) < 32, x, 0.0)
    high = kept.astype(bf16).astype(f32)
    return high + lane_roll(kept - high, 32)


def fold_pairs(x):
    return x + lane_roll(x, -32)


def gather_kernel(ids_ref, table_ref, out_ref):
    rows = table_ref.shape[0]
    count = ids_ref.shape[1]
    hot = jnp.where(iota((rows, count), 0) == ids_ref[...], 1.0, 0.0).astype(bf16)
    out_ref[...] = dot(hot, table_ref[...], TN).astype(bf16)


def scatter_kernel(ids_ref, grads_ref, out_ref):
    rows = out_ref.shape[0]
    count = ids_ref.shape[1]
    hot = jnp.where(iota((rows, count), 0) == ids_ref[...], 1.0, 0.0).astype(bf16)
    total = dot(hot, grads_ref[...])
    out_ref[:, : 4 * F] = total[:, : 4 * F].astype(bf16)
    out_ref[:, 4 * F :] = split_pairs(fold_pairs(total[:, 4 * F :])).astype(bf16)


def sum_kernel(parts_ref, out_ref):
    total = parts_ref[0].astype(f32)
    for n in range(1, parts_ref.shape[0]):
        total = total + parts_ref[n].astype(f32)
    pairs = split_pairs(fold_pairs(total[:, 4 * F :]))
    total = jnp.concatenate([total[:, : 4 * F], pairs], axis=1).astype(bf16)
    for n in range(out_ref.shape[0]):
        out_ref[n] = total


def slot_permutation(slices, slots):
    count = slices * slots
    row, column = iota((count, count), 0), iota((count, count), 1)
    slot, place = row // slices, row % slices
    piece = (place % 8) * 4 + place // 8
    return jnp.where(column == piece * slots + slot, 1.0, 0.0).astype(bf16)


VISIT = [(t % 4) * 4 + t // 4 for t in range(16)]


def tile_kernel(
    pads_ref, offset_ref, blocks_ref, grad_ref, image_ref, sent_ref,
    rows, perm, basis, moments, feats_t, coefs, weights, weights_b, ratios, deltas, sums, trans, below, back,
):
    tile = pl.program_id(0)
    slots = 2 * LIST
    slices = 32

    @pl.when(tile == 0)
    def _():
        perm[...] = slot_permutation(slices, slots)
        rows[...] = dot(perm[...], blocks_ref[...]).astype(bf16)
        term, pixel = iota((LANES, PIX), 0), iota((LANES, PIX), 1)
        across, down = (pixel % TILE_W - 16).astype(f32), (pixel // TILE_W - 16).astype(f32)
        kind = jnp.where(term < 24, term % 8, 7)
        value = jnp.where(
            kind == 0, 1.0,
            jnp.where(kind == 1, across,
            jnp.where(kind == 2, down,
            jnp.where(kind == 3, across * across,
            jnp.where(kind == 4, across * down,
            jnp.where(kind == 5, down * down, 0.0))))))
        basis[...] = value.astype(bf16)
        term, lane = iota((8, LANES), 0), iota((8, LANES), 1)
        x, u = (lane % TILE_W - 16).astype(f32), (lane // TILE_W + 16).astype(f32)
        pick = lambda *values: functools.reduce(
            lambda rest, kv: jnp.where(term == kv[0], kv[1], rest), enumerate(values), jnp.zeros_like(x)
        )
        moments[:, :LANES] = pick(1.0, x, u, x * x, x * u, u * u)
        moments[:, LANES : 2 * LANES] = pick(0.0, 0.0, -4.0, 0.0, -4.0 * x, -8.0 * u - 16.0)
        moments[:, 2 * LANES :] = pick(0.0, 0.0, 0.0, 0.0, 0.0, 32.0)

    live = LIST - pads_ref[0, tile]
    shift_x, shift_y = offset_ref[0, 0] - 16.5, offset_ref[0, 1] - 16.5
    sub = iota((8, LANES), 0)

    lane = iota((BLOCK, LANES), 1)
    own = (lane % 4) == (iota((BLOCK, LANES), 0) // 32)
    rank = jnp.where(iota((8, LANES), 1) // 4 == iota((8, LANES), 0), 1.0, 0.0).astype(bf16)

    def parameters(k):
        at = pl.multiple_of((tile * LIST + k) * slices, slices)
        piece = rows[pl.ds(at, slices), 4 * F :]
        spread = jnp.where(own, jnp.concatenate([piece] * 4, axis=0).astype(f32), 0.0).astype(bf16)
        table = dot(rank, spread, NT)
        cx, cy = table[0:1] + shift_x, table[1:2] + shift_y
        a, c = jnp.exp(table[2:3]), jnp.exp(table[3:4])
        root = jnp.exp(0.5 * (table[2:3] + table[3:4]))
        return cx, cy, a, c, root, table[4:5] * root, table[5:6]

    def features(k):
        at = pl.multiple_of((tile * LIST + k) * slices, slices)
        return jnp.concatenate(
            [rows[pl.ds(at, slices), F * i : F * (i + 1)] for i in range(4)], axis=0
        )

    trans[...] = jnp.ones_like(trans)
    below[...] = jnp.zeros_like(below)

    def forward(k, unused):
        cx, cy, a, c, root, b, logit = parameters(k)
        h = -0.5 * LOG2E
        level = -LOG2E * jnp.log(1.0 + jnp.exp(-logit))
        terms = jnp.concatenate(
            [
                jnp.where(k < live, h * (a * cx * cx + 2.0 * b * cx * cy + c * cy * cy) + level, -1e30),
                (-2.0 * h) * (a * cx + b * cy),
                (-2.0 * h) * (b * cx + c * cy),
                h * a,
                (2.0 * h) * b,
                h * c,
                jnp.zeros((2, LANES), f32),
            ],
            axis=0,
        )
        high = terms.astype(bf16).astype(f32)
        middle = (terms - high).astype(bf16).astype(f32)
        low = terms - high - middle
        coef = jnp.concatenate([high, middle, low, jnp.zeros((LANES - 24, LANES), f32)], axis=0)
        coef = coef.T.astype(bf16)
        first = pl.multiple_of(k * BLOCK, BLOCK)
        feats_t[:, pl.ds(first, BLOCK)] = features(k).astype(f32).T.astype(bf16)
        for chunk in range(CHUNKS):
            columns = slice(chunk * LANES, (chunk + 1) * LANES)
            alpha = jnp.exp2(dot(coef, basis[:, columns]))
            keep = 1.0 - alpha
            ratios[pl.ds(first, BLOCK), columns] = alpha / keep
            before, run = [None] * 16, None
            for v in VISIT:
                before[v] = run
                piece = keep[8 * v : 8 * v + 8]
                run = piece if run is None else run * piece
            for step in (1, 2, 4):
                run = run * jnp.where(sub >= step, pltpu.roll(run, step, 0), 1.0)
            carry = trans[8 * chunk : 8 * chunk + 8]
            start = carry * jnp.where(sub >= 1, pltpu.roll(run, 1, 0), 1.0)
            trans[8 * chunk : 8 * chunk + 8] = carry * jnp.broadcast_to(run[7:8], (8, LANES))
            out = []
            for v in range(16):
                reach = start if before[v] is None else start * before[v]
                out.append(alpha[8 * v : 8 * v + 8] * reach)
            weight = jnp.concatenate(out, axis=0)
            weights[pl.ds(first, BLOCK), columns] = weight
            weights_b[pl.ds(first, BLOCK), columns] = weight.astype(bf16)
        return unused

    lax.fori_loop(0, LIST, forward, 0)

    image_ref[0, 0] = dot(feats_t[...], weights_b[...]).T.astype(bf16)

    def backward(step, unused):
        k = LIST - 1 - step
        first = pl.multiple_of(k * BLOCK, BLOCK)
        feats = features(k)
        for chunk in range(CHUNKS):
            columns = slice(chunk * LANES, (chunk + 1) * LANES)
            slope = dot(feats, grad_ref[0, 0, columns, :], NT)
            gain = slope * weights[pl.ds(first, BLOCK), columns]
            after, run = [None] * 16, None
            for v in VISIT[::-1]:
                after[v] = run
                piece = gain[8 * v : 8 * v + 8]
                run = piece if run is None else run + piece
            for shift in (1, 2, 4):
                run = run + jnp.where(sub < 8 - shift, pltpu.roll(run, 8 - shift, 0), 0.0)
            carry = below[8 * chunk : 8 * chunk + 8]
            start = carry + jnp.where(sub < 7, pltpu.roll(run, 7, 0), 0.0)
            below[8 * chunk : 8 * chunk + 8] = carry + jnp.broadcast_to(run[0:1], (8, LANES))
            out = []
            for v in range(16):
                rest = start if after[v] is None else start + after[v]
                ratio = ratios[pl.ds(first + 8 * v, 8), columns]
                out.append(gain[8 * v : 8 * v + 8] - rest * ratio)
            deltas[:, columns] = jnp.concatenate(out, axis=0)
        for v in range(16):
            once = twice = thrice = None
            for chunk in range(CHUNKS):
                piece = deltas[8 * v : 8 * v + 8, chunk * LANES : (chunk + 1) * LANES]
                once = piece if once is None else once + piece
                twice = once if twice is None else twice + once
                thrice = twice if thrice is None else thrice + twice
            sums[8 * v : 8 * v + 8, :LANES] = once
            sums[8 * v : 8 * v + 8, LANES : 2 * LANES] = twice
            sums[8 * v : 8 * v + 8, 2 * LANES :] = thrice
        table = dot(moments[...], sums[...], NT, lax.Precision.HIGHEST)
        cx, cy, a, c, root, b, logit = parameters(k)
        m0, mx, my, mxx, mxy, myy = (table[n : n + 1] for n in range(6))
        dx, dy = mx - cx * m0, my - cy * m0
        dxx = mxx - 2.0 * cx * mx + cx * cx * m0
        dxy = mxy - cx * my - cy * mx + cx * cy * m0
        dyy = myy - 2.0 * cy * my + cy * cy * m0
        grads = jnp.concatenate(
            [
                a * dx + b * dy,
                b * dx + c * dy,
                -0.5 * (a * dxx + b * dxy),
                -0.5 * (c * dyy + b * dxy),
                -root * dxy,
                m0 / (1.0 + jnp.exp(logit)),
                jnp.zeros((2, LANES), f32),
            ],
            axis=0,
        )
        high = grads.astype(bf16).astype(f32)
        low = grads - high
        group = iota((8, LANES), 1) // 32
        both = [jnp.where(group == i, part, 0.0) for part in (high, low) for i in range(4)]
        both.append(jnp.zeros((LANES - 64, LANES), f32))
        turned = jnp.concatenate(both, axis=0).T
        packed = turned[0:32] + turned[32:64] + turned[64:96] + turned[96:128]
        pulled = dot(weights_b[pl.ds(first, BLOCK), :], grad_ref[0, 0])
        at = pl.multiple_of((tile * LIST + k) * slices, slices)
        for i in range(4):
            back[pl.ds(at, slices), F * i : F * (i + 1)] = pulled[32 * i : 32 * i + 32].astype(bf16)
        back[pl.ds(at, slices), 4 * F :] = packed.astype(bf16)
        return unused

    lax.fori_loop(0, LIST, backward, 0)

    @pl.when(tile == 1)
    def _():
        sent_ref[...] = dot(perm[...], back[...], TN).astype(bf16)


def in_vmem(kernel, out_shape, *args):
    spec = pl.BlockSpec(memory_space=pltpu.VMEM)
    return pl.pallas_call(
        kernel, out_shape=out_shape, in_specs=[spec] * len(args), out_specs=spec
    )(*args)


def tile_call(pads, offset, blocks, grad):
    count = blocks.shape[0]
    smem = pl.BlockSpec(memory_space=pltpu.SMEM)
    whole = pl.BlockSpec((count, WIDTH), lambda t: (0, 0))
    image = pl.BlockSpec((1, 1, PIX, F), lambda t: (0, t, 0, 0))
    every = LIST * BLOCK
    return pl.pallas_call(
        tile_kernel,
        grid=(2,),
        out_shape=(
            jax.ShapeDtypeStruct(grad.shape, bf16),
            jax.ShapeDtypeStruct((count, WIDTH), bf16),
        ),
        in_specs=[smem, smem, whole, image],
        out_specs=(image, whole),
        scratch_shapes=[
            pltpu.VMEM((count, WIDTH), bf16),
            pltpu.VMEM((count, count), bf16),
            pltpu.VMEM((LANES, PIX), bf16),
            pltpu.VMEM((8, 3 * LANES), f32),
            pltpu.VMEM((F, every), bf16),
            pltpu.VMEM((8, LANES), f32),
            pltpu.VMEM((every, PIX), f32),
            pltpu.VMEM((every, PIX), bf16),
            pltpu.VMEM((every, PIX), f32),
            pltpu.VMEM((BLOCK, PIX), f32),
            pltpu.VMEM((BLOCK, 3 * LANES), f32),
            pltpu.VMEM((8 * CHUNKS, LANES), f32),
            pltpu.VMEM((8 * CHUNKS, LANES), f32),
            pltpu.VMEM((count, WIDTH), bf16),
        ],
        compiler_params=pltpu.CompilerParams(vmem_limit_bytes=48 * 1024 * 1024),
    )(pads, offset, blocks, grad)


def shards(
    centers,
    log_scales,
    correlation,
    opacity_logit,
    features,
    view_offset,
    block_list,
    pad_count,
    block_home,
    image_grad,
):
    views, tiles = lax.axis_size("view"), lax.axis_size("tile")
    held = centers.shape[0]
    total = held * tiles
    part = BLOCK // views
    view = lax.axis_index("view")

    def exchange(x, axis):
        return lax.all_to_all(x, axis, split_axis=0, concat_axis=0, tiled=True)

    rows = jnp.take(block_home, block_list.reshape(-1))
    slots = rows.shape[0]
    ids = exchange(jnp.broadcast_to(rows[None], (views, slots)), "view").reshape(1, -1)
    small = jnp.concatenate(
        [centers, log_scales, correlation[:, None], opacity_logit[:, None]], axis=1
    )
    small = lax.dynamic_slice_in_dim(small, view * part, part, axis=2).reshape(held, -1)
    mine = lax.dynamic_slice_in_dim(features, view * part, part, axis=1).reshape(held, -1)
    fill = jnp.zeros((held, WIDTH - part * F - small.shape[1]), bf16)
    slab = jnp.concatenate([mine, small, fill], axis=1)
    slab = jnp.broadcast_to(slab[None], (tiles, held, WIDTH)).reshape(total, WIDTH)
    table = exchange(slab, "tile")
    wanted = in_vmem(gather_kernel, jax.ShapeDtypeStruct((views * slots, WIDTH), bf16), ids, table)
    blocks = exchange(wanted, "view")

    image, sent = tile_call(pad_count, view_offset, blocks, image_grad)

    came = exchange(sent, "view")
    partial = in_vmem(scatter_kernel, jax.ShapeDtypeStruct((total, WIDTH), bf16), ids, came)
    partial = exchange(partial, "tile").reshape(tiles, held, WIDTH)
    slab = in_vmem(sum_kernel, jax.ShapeDtypeStruct((views, held, WIDTH), bf16), partial)
    slab = exchange(slab, "view")

    grads = slab[:, :, : part * F].reshape(views, held, part, F).transpose(1, 0, 2, 3)
    grad_features = grads.reshape(held, BLOCK, F).astype(f32)
    pairs = slab[:, :, part * F :].astype(f32)
    pairs = pairs[:, :, : part * PARAMS] + pairs[:, :, part * PARAMS : 2 * part * PARAMS]
    pairs = pairs.reshape(views, held, part, PARAMS).transpose(1, 3, 0, 2)
    pairs = pairs.reshape(held, PARAMS, BLOCK)
    return (image, pairs[:, 0:2], pairs[:, 2:4], pairs[:, 4], pairs[:, 5], grad_features)


def solution(mesh):
    in_specs = (
        P("tile", None, None),
        P("tile", None, None),
        P("tile", None),
        P("tile", None),
        P("tile", None, None),
        P("view", None),
        P("view", "tile", None),
        P("view", "tile"),
        P(),
        P("view", "tile", None, None),
    )
    out_specs = (
        P("view", "tile", None, None),
        P("tile", None, None),
        P("tile", None, None),
        P("tile", None),
        P("tile", None),
        P("tile", None, None),
    )
    return jax.shard_map(shards, mesh=mesh, in_specs=in_specs, out_specs=out_specs, check_vma=False)
```

time: 976 us -> 202 us (0.21)
  other arithmetic: 280 us -> 1.98 us
  local copies, waits for them, and re-layouts: 256 us -> 15.8 us
  waiting for transfers between devices: 174 us -> 24.2 us
  matrix products: 82.2 us -> 0 us
  blocking collectives: 141 us -> 95.3 us
  Pallas kernels: 0 us -> 39.2 us
  starting transfers between devices: 3.87 us -> 23.5 us
  between operations: 16.2 us -> 0.76 us
  loops' own time: 14.9 us -> 0 us
    another operation x67 -> x0, other arithmetic: 157 us -> none  [the longest x48 157 us: block_step(): before = jnp.cumsum(log_keep, axis=1) - log_keep]
    psum x1 -> x0, waiting for transfers between devices: 130 us -> none  [packed_total(): running = lax.psum(jnp.concatenate([a.ravel() for a in arrays]), axis)]
    dynamic_update_slice x96 -> x0, local copies, waits for them, and re-layouts: 122 us -> none  [render_tile(): lax.scan(jax.checkpoint(block_step), start_state, tuple(tensors) + (alive...]
    dot_general x58 -> x0, matrix products: 82.2 us -> none  [the longest x48 74.8 us: block_step(): jnp.dot(weight, feature.astype(jnp.bfloat16), preferred_element_type=jnp....]
    all_to_all x2 -> x4, blocking collectives: 141 us -> 95.3 us  [exchange(): return lax.all_to_all(x, axis, split_axis=0, concat_axis=0, tiled=True)]
    pallas_call x0 -> x4, Pallas kernels: none -> 39.2 us  [the longest x1 32.1 us: tile_call(): pl.pallas_call(tile_kernel, grid=(2,), out_shape=(jax.ShapeDtypeStruct(gr...]
    log1p x32 -> x0, other arithmetic: 36.5 us -> none  [block_step(): log_keep = jnp.log1p(-alphas)]
    reduce_sum x18 -> x0, other arithmetic: 32.5 us -> none  [the longest x16 32.2 us: block_step(): coef_c[None, :] * delta_y * delta_y]
  transfers between devices with their start and end apart: 2 -> 2, of which waited for: 2 -> 2; matrix products, arithmetic and copies ran while one was open for 0% -> 2% of each run, Pallas kernels for 0% -> 0%
where the time goes in v1:
time: 202 us; the launch traced here: 201 us
  blocking collectives  95.3 us (47%)
  Pallas kernels  39.2 us (19%)
  waiting for transfers between devices  24.2 us (12%)
  starting transfers between devices  23.5 us (12%)
  local copies, waits for them, and re-layouts  15.8 us (8%)
    all_to_all x4, blocking collectives, exchange(): return lax.all_to_all(x, axis, split_axis=0, concat_axis=0, tiled=True)  95.3 us
    pallas_call x1, Pallas kernels, tile_call(): pl.pallas_call(tile_kernel, grid=(2,), out_shape=(jax.ShapeDtypeStruct(gr...  32.1 us
    all_to_all x2, waiting for transfers between devices, exchange(): return lax.all_to_all(x, axis, split_axis=0, concat_axis=0, tiled=True)  24.2 us
    all_to_all x2, starting transfers between devices, exchange(): return lax.all_to_all(x, axis, split_axis=0, concat_axis=0, tiled=True)  23.5 us
    pallas_call x3, Pallas kernels, in_vmem(): pl.pallas_call(kernel, out_shape=out_shape, in_specs=[spec] * len(args),...  7.15 us
    convert_element_type x2, local copies, waits for them, and re-layouts, shards(): grad_features = grads.reshape(held, BLOCK, F).astype(f32)  4.64 us
  transfers between devices with their start and end apart: 2, of which 2 were waited for; matrix products, arithmetic and copies ran while one was open for 2% of the time, Pallas kernels for 0%

profile of v1, /device:TPU:1, one launch (start us, length us, event | category | flops | bytes accessed | tf_op | source)
XLA Modules:
  0.0 200.9 jit_solution(12413794937355356341)
XLA Ops:
  0.6 0.0 copy-start
  0.6 0.8 reshape.112
  1.5 0.8 reshape.111
  2.3 1.3 gather_fusion
  3.6 0.6 broadcast_in_dim.12
  4.2 10.3 %all-to-all-start = ((s32[32,1,16]{2,1,0:T(1,128)}), s32[32,1,16]{2,1,0:T(1,128)S(1)}, u32[]{:S(2)}, u32[]{:S(2)}) async-start(s32[32,1,16]{2,1,0:T(1,128)} %broadcast_in_dim.12), calls=%async_computation | async-start | bytes 32768 | tf_op jit(solution)/shard_map/all_to_all | solution.py:332
  14.6 0.7 copy.33
  15.3 0.7 copy.34
  16.0 0.9 dynamic-slice_maximum_fusion
  16.9 0.1 copy.35
  17.0 0.1 copy.36
  17.1 0.0 copy-done
  17.1 0.1 pad.2.clone
  17.2 4.3 %all-to-all-done = s32[32,1,16]{2,1,0:T(1,128)S(1)} async-done(((s32[32,1,16]{2,1,0:T(1,128)}), s32[32,1,16]{2,1,0:T(1,128)S(1)}, u32[]{:S(2)}, u32[]{:S(2)}) %all-to-all-start) | async-done | bytes 2080 | tf_op jit(solution)/shard_map/all_to_all | solution.py:332
  21.6 0.8 broadcast_in_dim.27
  22.4 0.0 copy-start.1
  22.4 0.0 copy-start.2
  22.4 0.0 copy-start.3
  22.4 13.2 %all-to-all-start.1 = ((bf16[16,24,640]{2,1,0:T(8,128)(2,1)}), bf16[16,24,640]{2,1,0:T(8,128)(2,1)S(1)}, u32[]{:S(2)}, u32[]{:S(2)}) async-start(bf16[16,24,640]{2,1,0:T(8,128)(2,1)} %broadcast_in_dim.27), calls=%async_computation.1 | async-start | bytes 983040 | tf_op jit(solution)/shard_map/all_to_all | solution.py:332
  35.6 0.5 broadcast.68
  36.1 0.7 reduce.3
  36.8 0.7 reshape.113.ids_ref
  37.5 19.9 %all-to-all-done.1 = bf16[16,24,640]{2,1,0:T(8,128)(2,1)S(1)} async-done(((bf16[16,24,640]{2,1,0:T(8,128)(2,1)}), bf16[16,24,640]{2,1,0:T(8,128)(2,1)S(1)}, u32[]{:S(2)}, u32[]{:S(2)}) %all-to-all-start.1) | async-done | bytes 491552 | tf_op jit(solution)/shard_map/all_to_all | solution.py:332
  57.3 0.0 copy-start.4
  57.3 0.8 copy-done.4
  58.1 2.5 %shard_map.145 = bf16[512,640]{1,0:T(8,128)(2,1)} custom-call(s32[1,512]{1,0:T(1,128)} %reshape.113.ids_ref, bf16[384,640]{1,0:T(8,128)(2,1)} %bitcast.29), custom_call_target="tpu_custom_call" | custom-call | tf_op jit(solution)/shard_map/pallas_call | solution.py:273
  60.6 23.9 %all_to_all.50 = bf16[32,16,640]{2,1,0:T(8,128)(2,1)S(1)} all-to-all(bf16[32,16,640]{2,1,0:T(8,128)(2,1)} %bitcast.28), channel_id=1, replica_groups=mesh['view'=32,'tile'=16] {'view'}, dimensions={0} | all-to-all | bytes 1310720 | tf_op jit(solution)/shard_map/all_to_all | solution.py:332
  84.5 0.0 copy-done.1
  84.5 0.0 copy-done.2
  84.5 0.0 copy-done.3
  84.5 32.1 %shard_map.146 = (bf16[1,2,1024,128]{3,2,1,0:T(8,128)(2,1)}, bf16[512,640]{1,0:T(8,128)(2,1)S(1)}) custom-call(s32[1,2]{1,0:T(1,128)S(1)} %copy-done.2, f32[1,2]{1,0:T(1,128)S(1)} %copy-done.3, bf16[512,640]{1,0:T(8,128)(2,1)S(1)} %bitcast.24, bf16[1,2,1024,128]{3,2,1,0:T(8,128)(2,1)S(1)} %copy-done.1), custom_call_target="tpu_custom_call" | custom-call | tf_op jit(solution)/shard_map/pallas_call | solution.py:284
  116.5 16.7 %all_to_all.51 = bf16[32,16,640]{2,1,0:T(8,128)(2,1)} all-to-all(bf16[32,16,640]{2,1,0:T(8,128)(2,1)S(1)} %bitcast.25), channel_id=1, replica_groups=mesh['view'=32,'tile'=16] {'view'}, dimensions={0} | all-to-all | bytes 1310720 | tf_op jit(solution)/shard_map/all_to_all | solution.py:332
  133.3 2.5 %shard_map.147 = bf16[384,640]{1,0:T(8,128)(2,1)} custom-call(s32[1,512]{1,0:T(1,128)} %reshape.113.ids_ref, bf16[512,640]{1,0:T(8,128)(2,1)} %bitcast.27), custom_call_target="tpu_custom_call" | custom-call | tf_op jit(solution)/shard_map/pallas_call | solution.py:273
  135.8 27.4 %all_to_all.52.parts_ref = bf16[16,24,640]{2,1,0:T(8,128)(2,1)} all-to-all(bf16[16,24,640]{2,1,0:T(8,128)(2,1)} %bitcast.30), channel_id=1, replica_groups=mesh['view'=32,'tile'=16] {'tile'}, dimensions={0} | all-to-all | bytes 983040 | tf_op jit(solution)/shard_map/all_to_all | solution.py:332
  163.2 2.2 %shard_map.148 = bf16[32,24,640]{2,1,0:T(8,128)(2,1)} custom-call(bf16[16,24,640]{2,1,0:T(8,128)(2,1)} %all_to_all.52.parts_ref), custom_call_target="tpu_custom_call" | custom-call | tf_op jit(solution)/shard_map/pallas_call | solution.py:273
  165.4 27.3 %all_to_all.53 = bf16[32,24,640]{2,1,0:T(8,128)(2,1)S(1)} all-to-all(bf16[32,24,640]{2,1,0:T(8,128)(2,1)} %shard_map.148), channel_id=1, replica_groups=mesh['view'=32,'tile'=16] {'view'}, dimensions={0} | all-to-all | bytes 1966080 | tf_op jit(solution)/shard_map/all_to_all | solution.py:332
  192.7 0.2 slice_add_fusion
  192.9 0.2 copy.44
  193.1 0.1 fusion.1
  193.2 0.1 fusion.2
  193.3 0.7 copy.41
  194.0 0.7 copy.43
  194.7 0.7 copy.42
  195.3 0.7 copy.40
  196.0 0.2 slice_convert_fusion
  196.2 1.7 reshape.119
  197.9 3.0 %copy.39 = f32[24,32,4,128]{3,2,1,0:T(4,128)} copy(f32[24,32,4,128]{3,2,0,1:T(4,128)} %bitcast.26) | data formatting | bytes 3145728 | tf_op jit(solution)/shard_map/convert_element_type | solution.py:358
  (8 shorter events, 0.1 us)
Async XLA Ops:
  0.6 16.4 %copy-start = (bf16[24,128,128]{2,1,0:T(8,128)(2,1)S(1)}, bf16[24,128,128]{2,1,0:T(8,128)(2,1)}, u32[]{:S(2)}) copy-start(bf16[24,128,128]{2,1,0:T(8,128)(2,1)} %param.14) | copy-start | bytes 2359300
  4.2 17.3 %all-to-all-start = ((s32[32,1,16]{2,1,0:T(1,128)}), s32[32,1,16]{2,1,0:T(1,128)S(1)}, u32[]{:S(2)}, u32[]{:S(2)}) async-start(s32[32,1,16]{2,1,0:T(1,128)} %broadcast_in_dim.12), calls=%async_computation | async-start | bytes 32768 | tf_op jit(solution)/shard_map/all_to_all | solution.py:332
  22.4 62.1 %copy-start.1 = (bf16[1,2,1024,128]{3,2,1,0:T(8,128)(2,1)S(1)}, bf16[1,2,1024,128]{3,2,1,0:T(8,128)(2,1)}, u32[]{:S(2)}) copy-start(bf16[1,2,1024,128]{3,2,1,0:T(8,128)(2,1)} %grad_ref.1) | copy-start | bytes 1572868
  22.4 62.1 %copy-start.2 = (s32[1,2]{1,0:T(1,128)S(1)}, s32[1,2]{1,0:T(1,128)}, u32[]{:S(2)}) copy-start(s32[1,2]{1,0:T(1,128)} %pads_ref.1) | copy-start | bytes 28
  22.4 62.1 %copy-start.3 = (f32[1,2]{1,0:T(1,128)S(1)}, f32[1,2]{1,0:T(1,128)}, u32[]{:S(2)}) copy-start(f32[1,2]{1,0:T(1,128)} %offset_ref.1) | copy-start | bytes 28
  22.4 35.0 %all-to-all-start.1 = ((bf16[16,24,640]{2,1,0:T(8,128)(2,1)}), bf16[16,24,640]{2,1,0:T(8,128)(2,1)S(1)}, u32[]{:S(2)}, u32[]{:S(2)}) async-start(bf16[16,24,640]{2,1,0:T(8,128)(2,1)} %broadcast_in_dim.27), calls=%async_computation.1 | async-start | bytes 983040 | tf_op jit(solution)/shard_map/all_to_all | solution.py:332
  57.3 0.8 copy-start.4

commit v2 on v1

v2 whole, which is shorter than its diff:
```python
import functools

import jax
import jax.numpy as jnp
from jax import lax
from jax.experimental import pallas as pl
from jax.experimental.pallas import tpu as pltpu
from jax.sharding import PartitionSpec as P


TILE_W = 32
PIX = 1024
F = 128
BLOCK = 128
LIST = 8
LANES = 128
WIDTH = 640
LOG2E = 1.4426950408889634
CHUNKS = PIX // LANES
UNROLL = 2
f32 = jnp.float32
bf16 = jnp.bfloat16

NN = (((1,), (0,)), ((), ()))
NT = (((1,), (1,)), ((), ()))
TN = (((0,), (0,)), ((), ()))


def dot(a, b, dims=NN, precision=None):
    return lax.dot_general(a, b, dims, precision=precision, preferred_element_type=f32)


def iota(shape, dim):
    return lax.broadcasted_iota(jnp.int32, shape, dim)


def lane_roll(x, shift):
    return pltpu.roll(x, shift % LANES, 1)


def split_pairs(x):
    kept = jnp.where(iota(x.shape, 1) < 32, x, 0.0)
    high = kept.astype(bf16).astype(f32)
    return high + lane_roll(kept - high, 32)


def fold_pairs(x):
    return x + lane_roll(x, -32)


def gather_kernel(ids_ref, table_ref, out_ref):
    rows = table_ref.shape[0]
    count = ids_ref.shape[1]
    hot = jnp.where(iota((rows, count), 0) == ids_ref[...], 1.0, 0.0).astype(bf16)
    out_ref[...] = dot(hot, table_ref[...], TN).astype(bf16)


def scatter_kernel(ids_ref, grads_ref, out_ref):
    rows = out_ref.shape[0]
    count = ids_ref.shape[1]
    hot = jnp.where(iota((rows, count), 0) == ids_ref[...], 1.0, 0.0).astype(bf16)
    total = dot(hot, grads_ref[...])
    out_ref[:, : 4 * F] = total[:, : 4 * F].astype(bf16)
    out_ref[:, 4 * F :] = split_pairs(fold_pairs(total[:, 4 * F :])).astype(bf16)


def sum_kernel(parts_ref, out_ref):
    total = parts_ref[0].astype(f32)
    for n in range(1, parts_ref.shape[0]):
        total = total + parts_ref[n].astype(f32)
    pairs = split_pairs(fold_pairs(total[:, 4 * F :]))
    total = jnp.concatenate([total[:, : 4 * F], pairs], axis=1).astype(bf16)
    for n in range(out_ref.shape[0]):
        out_ref[n] = total


def slot_permutation(slices, slots):
    count = slices * slots
    row, column = iota((count, count), 0), iota((count, count), 1)
    slot, place = row // slices, row % slices
    piece = (place % 8) * 4 + place // 8
    return jnp.where(column == piece * slots + slot, 1.0, 0.0).astype(bf16)


VISIT = [(t % 4) * 4 + t // 4 for t in range(16)]
EVERY = LIST * BLOCK


def tile_kernel(
    pads_ref, offset_ref, blocks_ref, grad_ref, image_ref, sent_ref,
    rows, perm, basis, moments, feats, feats_t, coefs, weights, weights_b, ratios, deltas, sums, trans, below, back,
):
    tile = pl.program_id(0)
    slots = 2 * LIST
    slices = 32

    @pl.when(tile == 0)
    def _():
        perm[...] = slot_permutation(slices, slots)
        rows[...] = dot(perm[...], blocks_ref[...]).astype(bf16)
        term, pixel = iota((LANES, PIX), 0), iota((LANES, PIX), 1)
        across, down = (pixel % TILE_W - 16).astype(f32), (pixel // TILE_W - 16).astype(f32)
        kind = jnp.where(term < 24, term % 8, 7)
        value = jnp.where(
            kind == 0, 1.0,
            jnp.where(kind == 1, across,
            jnp.where(kind == 2, down,
            jnp.where(kind == 3, across * across,
            jnp.where(kind == 4, across * down,
            jnp.where(kind == 5, down * down, 0.0))))))
        basis[...] = value.astype(bf16)
        term, lane = iota((16, LANES), 0), iota((16, LANES), 1)
        x, y = (lane % TILE_W - 16).astype(f32), (lane // TILE_W).astype(f32)
        one = jnp.ones_like(x)
        pick = lambda first, *values: functools.reduce(
            lambda rest, kv: jnp.where(term == kv[0], kv[1], rest),
            enumerate(values, first), jnp.zeros_like(x),
        )
        moments[:, :LANES] = pick(0, one, x, y, x * x, x * y, y * y).astype(bf16)
        moments[:, LANES : 2 * LANES] = pick(6, one, x, y).astype(bf16)
        moments[:, 2 * LANES :] = pick(9, one).astype(bf16)

    live = LIST - pads_ref[0, tile]
    shift_x, shift_y = offset_ref[0, 0] - 16.5, offset_ref[0, 1] - 16.5
    sub = iota((8, LANES), 0)

    lane = iota((BLOCK, LANES), 1)
    own = (lane % 4) == (iota((BLOCK, LANES), 0) // 32)
    rank = jnp.where(iota((8, LANES), 1) // 4 == iota((8, LANES), 0), 1.0, 0.0).astype(bf16)
    spread = []
    for k in range(LIST):
        at = pl.multiple_of((tile * LIST + k) * slices, slices)
        piece = rows[pl.ds(at, slices), 4 * F :]
        piece = jnp.concatenate([piece] * 4, axis=0).astype(f32)
        spread.append(jnp.where(own, piece, 0.0).astype(bf16))
        feat = jnp.concatenate(
            [rows[pl.ds(at, slices), F * i : F * (i + 1)] for i in range(4)], axis=0
        )
        feats[BLOCK * k : BLOCK * (k + 1), :] = feat
        feats_t[:, BLOCK * k : BLOCK * (k + 1)] = feat.astype(f32).T.astype(bf16)
    table = dot(rank, jnp.concatenate(spread, axis=0), NT)
    cx, cy = table[0:1] + shift_x, table[1:2] + shift_y
    a, c = jnp.exp(table[2:3]), jnp.exp(table[3:4])
    root = jnp.exp(0.5 * (table[2:3] + table[3:4]))
    b, logit = table[4:5] * root, table[5:6]

    h = -0.5 * LOG2E
    level = -LOG2E * jnp.log(1.0 + jnp.exp(-logit))
    level = level + h * (a * cx * cx + 2.0 * b * cx * cy + c * cy * cy)
    terms = jnp.concatenate(
        [
            jnp.where(iota((1, EVERY), 1) // BLOCK < live, level, -1e30),
            (-2.0 * h) * (a * cx + b * cy),
            (-2.0 * h) * (b * cx + c * cy),
            h * a,
            (2.0 * h) * b,
            h * c,
            jnp.zeros((2, EVERY), f32),
        ],
        axis=0,
    )
    high = terms.astype(bf16).astype(f32)
    middle = (terms - high).astype(bf16).astype(f32)
    parts = [high, middle, terms - high - middle]
    for k in range(LIST):
        square = [part[:, BLOCK * k : BLOCK * (k + 1)] for part in parts]
        square = jnp.concatenate(square + [jnp.zeros((LANES - 24, LANES), f32)], axis=0)
        coefs[BLOCK * k : BLOCK * (k + 1), :] = square.T.astype(bf16)

    trans[...] = jnp.ones_like(trans)
    below[...] = jnp.zeros_like(below)

    def forward(k):
        first = pl.multiple_of(k * BLOCK, BLOCK)
        coef = coefs[pl.ds(first, BLOCK), :]
        for chunk in range(CHUNKS):
            columns = slice(chunk * LANES, (chunk + 1) * LANES)
            alpha = jnp.exp2(dot(coef, basis[:, columns]))
            keep = 1.0 - alpha
            ratios[pl.ds(first, BLOCK), columns] = alpha / keep
            before, run = [None] * 16, None
            for v in VISIT:
                before[v] = run
                piece = keep[8 * v : 8 * v + 8]
                run = piece if run is None else run * piece
            for step in (1, 2, 4):
                run = run * jnp.where(sub >= step, pltpu.roll(run, step, 0), 1.0)
            carry = trans[8 * chunk : 8 * chunk + 8]
            start = carry * jnp.where(sub >= 1, pltpu.roll(run, 1, 0), 1.0)
            trans[8 * chunk : 8 * chunk + 8] = carry * jnp.broadcast_to(run[7:8], (8, LANES))
            out = []
            for v in range(16):
                reach = start if before[v] is None else start * before[v]
                out.append(alpha[8 * v : 8 * v + 8] * reach)
            weight = jnp.concatenate(out, axis=0)
            weights[pl.ds(first, BLOCK), columns] = weight
            weights_b[pl.ds(first, BLOCK), columns] = weight.astype(bf16)

    def backward(k):
        first = pl.multiple_of(k * BLOCK, BLOCK)
        feat = feats[pl.ds(first, BLOCK), :]
        for chunk in range(CHUNKS):
            columns = slice(chunk * LANES, (chunk + 1) * LANES)
            slope = dot(feat, grad_ref[0, 0, columns, :], NT)
            gain = slope * weights[pl.ds(first, BLOCK), columns]
            after, run = [None] * 16, None
            for v in VISIT[::-1]:
                after[v] = run
                piece = gain[8 * v : 8 * v + 8]
                run = piece if run is None else run + piece
            for shift in (1, 2, 4):
                run = run + jnp.where(sub < 8 - shift, pltpu.roll(run, 8 - shift, 0), 0.0)
            carry = below[8 * chunk : 8 * chunk + 8]
            start = carry + jnp.where(sub < 7, pltpu.roll(run, 7, 0), 0.0)
            below[8 * chunk : 8 * chunk + 8] = carry + jnp.broadcast_to(run[0:1], (8, LANES))
            out = []
            for v in range(16):
                rest = start if after[v] is None else start + after[v]
                ratio = ratios[pl.ds(first + 8 * v, 8), columns]
                out.append(gain[8 * v : 8 * v + 8] - rest * ratio)
            deltas[:, columns] = jnp.concatenate(out, axis=0)
        for v in range(16):
            once = twice = thrice = None
            for chunk in range(CHUNKS):
                piece = deltas[8 * v : 8 * v + 8, chunk * LANES : (chunk + 1) * LANES]
                once = piece if once is None else once + piece
                twice = once if twice is None else twice + once
                thrice = twice if thrice is None else thrice + twice
            at = pl.ds(first + 8 * v, 8)
            sums[at, :LANES] = once
            sums[at, LANES : 2 * LANES] = twice
            sums[at, 2 * LANES :] = thrice

    def both(step, entry):
        for n in range(UNROLL):
            entry(step * UNROLL + n)

    lax.fori_loop(0, LIST // UNROLL, lambda step, u: (both(step, forward), u)[1], 0)
    image_ref[0, 0] = dot(feats_t[...], weights_b[...]).T.astype(bf16)
    lax.fori_loop(
        0, LIST // UNROLL, lambda step, u: (both(step, lambda n: backward(LIST - 1 - n)), u)[1], 0
    )

    pulled = dot(weights_b[...], grad_ref[0, 0]).astype(bf16)
    high = sums[...].astype(bf16)
    middle = (sums[...] - high.astype(f32)).astype(bf16)
    table = dot(moments[...], high, NT) + dot(moments[...], middle, NT)
    s, sx, sy, sxx, sxy, syy, t, tx, ty, w = (table[n : n + 1] for n in range(10))
    m0, mx, mxx = s, sx, sxx
    my = sy + 16.0 * s - 4.0 * t
    mxy = sxy + 16.0 * sx - 4.0 * tx
    myy = syy + 32.0 * sy + 256.0 * s - 8.0 * ty - 144.0 * t + 32.0 * w
    dx, dy = mx - cx * m0, my - cy * m0
    dxx = mxx - 2.0 * cx * mx + cx * cx * m0
    dxy = mxy - cx * my - cy * mx + cx * cy * m0
    dyy = myy - 2.0 * cy * my + cy * cy * m0
    grads = jnp.concatenate(
        [
            a * dx + b * dy,
            b * dx + c * dy,
            -0.5 * (a * dxx + b * dxy),
            -0.5 * (c * dyy + b * dxy),
            -root * dxy,
            m0 / (1.0 + jnp.exp(logit)),
            jnp.zeros((2, EVERY), f32),
        ],
        axis=0,
    )
    high = grads.astype(bf16).astype(f32)
    low = grads - high
    group = iota((8, LANES), 1) // 32
    for k in range(LIST):
        pair = [part[:, BLOCK * k : BLOCK * (k + 1)] for part in (high, low)]
        pair = [jnp.where(group == i, part, 0.0) for part in pair for i in range(4)]
        pair.append(jnp.zeros((LANES - 64, LANES), f32))
        turned = jnp.concatenate(pair, axis=0).T
        packed = turned[0:32] + turned[32:64] + turned[64:96] + turned[96:128]
        at = pl.multiple_of((tile * LIST + k) * slices, slices)
        for i in range(4):
            first = BLOCK * k + 32 * i
            back[pl.ds(at, slices), F * i : F * (i + 1)] = pulled[first : first + 32]
        back[pl.ds(at, slices), 4 * F :] = packed.astype(bf16)

    @pl.when(tile == 1)
    def _():
        sent_ref[...] = dot(perm[...], back[...], TN).astype(bf16)


def finish_kernel(slab_ref, centers_ref, scales_ref, corr_ref, opac_ref, feats_ref, wide, tall):
    slices, held = slab_ref.shape[0], slab_ref.shape[1]
    for n in range(slices):
        for i in range(5):
            wide[i, held * n : held * (n + 1), :] = slab_ref[n, :, F * i : F * (i + 1)].astype(f32)
    lane = iota((slices, LANES), 1)
    place = jnp.where(lane < 64, (lane % 32) // 8, -1)
    for n in range(held):
        at = pl.ds(n, slices, stride=held)
        small = wide[4, at, :]
        for i in range(4):
            feats_ref[n, pl.ds(i, slices, stride=4), :] = wide[i, at, :]
            tall[pl.ds(BLOCK * n + i, slices, stride=4), :] = jnp.where(place == i, small, 0.0)
    rank = jnp.where(iota((8, LANES), 1) % 8 == iota((8, LANES), 0), 1.0, 0.0).astype(bf16)
    table = dot(rank, tall[...].astype(bf16), NT)
    for n in range(held):
        own = table[:, BLOCK * n : BLOCK * (n + 1)]
        centers_ref[n] = own[0:2]
        scales_ref[n] = own[2:4]
        corr_ref[n : n + 1, :] = own[4:5]
        opac_ref[n : n + 1, :] = own[5:6]


def cut_kernel(view_ref, params_ref, feats_ref, out_ref):
    held = feats_ref.shape[0]
    view = view_ref[0]
    part = 4
    base = pl.multiple_of((view // 4) * 16, 16)
    near = feats_ref[:, pl.ds(base, 16), :].reshape(held * 16, F)
    row, column = iota((held, held * 16), 0), iota((held, held * 16), 1)
    cuts = []
    for i in range(part):
        hot = jnp.where(column == row * 16 + (view % 4) * part + i, 1.0, 0.0).astype(bf16)
        cuts.append(dot(hot, near))
    gauss, lane = iota((BLOCK, LANES), 0) - view * part, iota((BLOCK, LANES), 1)
    small = jnp.zeros((held, LANES), f32)
    for j in range(params_ref.shape[0]):
        chosen = (lane == gauss + part * j) & (gauss >= 0) & (gauss < part)
        small = small + dot(params_ref[j], jnp.where(chosen, 1.0, 0.0).astype(bf16))
    slab = jnp.concatenate(cuts + [small], axis=1).astype(bf16)
    for n in range(out_ref.shape[0]):
        out_ref[n] = slab


def in_vmem(kernel, shape, *args):
    spec = pl.BlockSpec(memory_space=pltpu.VMEM)
    return pl.pallas_call(
        kernel, out_shape=pltpu.VMEM(shape, bf16), in_specs=[spec] * len(args), out_specs=spec
    )(*args)


def tile_call(pads, offset, blocks, grad):
    count = blocks.shape[0]
    smem = pl.BlockSpec(memory_space=pltpu.SMEM)
    whole = pl.BlockSpec((count, WIDTH), lambda t: (0, 0))
    image = pl.BlockSpec((1, 1, PIX, F), lambda t: (0, t, 0, 0))
    return pl.pallas_call(
        tile_kernel,
        grid=(2,),
        out_shape=(
            jax.ShapeDtypeStruct(grad.shape, bf16),
            jax.ShapeDtypeStruct((count, WIDTH), bf16),
        ),
        in_specs=[smem, smem, whole, image],
        out_specs=(image, whole),
        scratch_shapes=[
            pltpu.VMEM((count, WIDTH), bf16),
            pltpu.VMEM((count, count), bf16),
            pltpu.VMEM((LANES, PIX), bf16),
            pltpu.VMEM((16, 3 * LANES), bf16),
            pltpu.VMEM((EVERY, F), bf16),
            pltpu.VMEM((F, EVERY), bf16),
            pltpu.VMEM((EVERY, LANES), bf16),
            pltpu.VMEM((EVERY, PIX), f32),
            pltpu.VMEM((EVERY, PIX), bf16),
            pltpu.VMEM((EVERY, PIX), f32),
            pltpu.VMEM((BLOCK, PIX), f32),
            pltpu.VMEM((EVERY, 3 * LANES), f32),
            pltpu.VMEM((8 * CHUNKS, LANES), f32),
            pltpu.VMEM((8 * CHUNKS, LANES), f32),
            pltpu.VMEM((count, WIDTH), bf16),
        ],
        compiler_params=pltpu.CompilerParams(vmem_limit_bytes=48 * 1024 * 1024),
    )(pads, offset, blocks, grad)


def shards(
    centers,
    log_scales,
    correlation,
    opacity_logit,
    features,
    view_offset,
    block_list,
    pad_count,
    block_home,
    image_grad,
):
    views, tiles = lax.axis_size("view"), lax.axis_size("tile")
    held = centers.shape[0]
    total = held * tiles
    view = lax.axis_index("view")

    def exchange(x, axis):
        return lax.all_to_all(x, axis, split_axis=0, concat_axis=0, tiled=True)

    params = jnp.stack(
        [centers[:, 0], centers[:, 1], log_scales[:, 0], log_scales[:, 1], correlation, opacity_logit]
    )
    spec = pl.BlockSpec(memory_space=pltpu.VMEM)
    slab = pl.pallas_call(
        cut_kernel,
        out_shape=jax.ShapeDtypeStruct((tiles, held, WIDTH), bf16),
        in_specs=[pl.BlockSpec(memory_space=pltpu.SMEM), spec, spec],
        out_specs=spec,
    )(view.reshape(1), params, features)
    table = exchange(slab, "tile")
    rows = jnp.take(block_home, block_list.reshape(-1))
    slots = rows.shape[0]
    asked = lax.all_gather(rows, "view")
    table, ids = table.reshape(total, WIDTH), asked.reshape(1, -1)
    wanted = in_vmem(gather_kernel, (views * slots, WIDTH), ids, table)
    blocks = exchange(wanted, "view")

    image, sent = tile_call(pad_count, view_offset, blocks, image_grad)

    came = exchange(sent, "view")
    partial = in_vmem(scatter_kernel, (total, WIDTH), ids, came)
    partial = exchange(partial, "tile").reshape(tiles, held, WIDTH)
    slab = in_vmem(sum_kernel, (views, held, WIDTH), partial)
    slab = exchange(slab, "view")

    shape = lambda *dims: jax.ShapeDtypeStruct(dims, f32)
    spec = pl.BlockSpec(memory_space=pltpu.VMEM)
    grads = pl.pallas_call(
        finish_kernel,
        out_shape=(
            shape(held, 2, BLOCK), shape(held, 2, BLOCK), shape(held, BLOCK), shape(held, BLOCK),
            shape(held, BLOCK, F),
        ),
        in_specs=[spec],
        out_specs=(spec,) * 5,
        scratch_shapes=[
            pltpu.VMEM((5, views * held, LANES), f32),
            pltpu.VMEM((held * BLOCK, LANES), f32),
        ],
    )(slab)
    return (image, *grads)


def solution(mesh):
    in_specs = (
        P("tile", None, None),
        P("tile", None, None),
        P("tile", None),
        P("tile", None),
        P("tile", None, None),
        P("view", None),
        P("view", "tile", None),
        P("view", "tile"),
        P(),
        P("view", "tile", None, None),
    )
    out_specs = (
        P("view", "tile", None, None),
        P("tile", None, None),
        P("tile", None, None),
        P("tile", None),
        P("tile", None),
        P("tile", None, None),
    )
    return jax.shard_map(shards, mesh=mesh, in_specs=in_specs, out_specs=out_specs, check_vma=False)
```

time: 202 us -> 170 us (0.84)
  waiting for transfers between devices: 24.2 us -> 0.01 us
  blocking collectives: 95.3 us -> 118 us
  Pallas kernels: 39.2 us -> 27.6 us
  local copies, waits for them, and re-layouts: 15.8 us -> 6.48 us
  starting transfers between devices: 23.5 us -> 15.7 us
    all_to_all x2 -> x1, waiting for transfers between devices: 24.2 us -> 0.01 us  [exchange(): return lax.all_to_all(x, axis, split_axis=0, concat_axis=0, tiled=True)]
    all_gather x0 -> x1, blocking collectives: none -> 22.6 us  [shards(): asked = lax.all_gather(rows, 'view')]
    pallas_call x1, Pallas kernels: 32.1 us -> 17.8 us  [tile_call(): pl.pallas_call(tile_kernel, grid=(2,), out_shape=(jax.ShapeDtypeStruct(gr...]
    all_to_all x2 -> x1, starting transfers between devices: 23.5 us -> 15.7 us  [exchange(): return lax.all_to_all(x, axis, split_axis=0, concat_axis=0, tiled=True)]
    convert_element_type x2 -> x0, local copies, waits for them, and re-layouts: 4.64 us -> none  [shards(): grad_features = grads.reshape(held, BLOCK, F).astype(f32)]
    broadcast_in_dim x5 -> x0, local copies, waits for them, and re-layouts: 2.85 us -> none  [the longest x1 0.82 us: shards(): jnp.broadcast_to(slab[None], (tiles, held, WIDTH)).reshape(total, WIDTH)]
    pallas_call x3 -> x5, Pallas kernels: 7.15 us -> 9.84 us  [the longest x3 4.59 us: in_vmem(): pl.pallas_call(kernel, out_shape=pltpu.VMEM(shape, bf16), in_specs=[spec]...]
  transfers between devices with their start and end apart: 2 -> 1, of which waited for: 2 -> 0; matrix products, arithmetic and copies ran while one was open for 2% -> 2% of each run, Pallas kernels for 0% -> 0%
where the time goes in v2:
time: 170 us; the launch traced here: 169 us
  blocking collectives  118 us (69%)
  Pallas kernels  27.6 us (16%)
  starting transfers between devices  15.7 us (9%)
  local copies, waits for them, and re-layouts  6.48 us (4%)
    all_to_all x4, blocking collectives, exchange(): return lax.all_to_all(x, axis, split_axis=0, concat_axis=0, tiled=True)  95.3 us
    all_gather x1, blocking collectives, shards(): asked = lax.all_gather(rows, 'view')  22.6 us
    pallas_call x1, Pallas kernels, tile_call(): pl.pallas_call(tile_kernel, grid=(2,), out_shape=(jax.ShapeDtypeStruct(gr...  17.8 us
    all_to_all x1, starting transfers between devices, exchange(): return lax.all_to_all(x, axis, split_axis=0, concat_axis=0, tiled=True)  15.7 us
    pallas_call x3, Pallas kernels, in_vmem(): pl.pallas_call(kernel, out_shape=pltpu.VMEM(shape, bf16), in_specs=[spec]...  4.59 us
  transfers between devices with their start and end apart: 1, of which 0 were waited for; matrix products, arithmetic and copies ran while one was open for 2% of the time, Pallas kernels for 0%

profile of v2, /device:TPU:1, one launch (start us, length us, event | category | flops | bytes accessed | tf_op | source)
XLA Modules:
  0.0 169.3 jit_solution(11088683337545919714)
XLA Ops:
  0.6 0.0 copy-start
  0.6 0.0 copy-start.6
  0.7 0.8 fusion.3
  1.5 0.8 fusion.2
  2.3 0.7 constant_dynamic-update-slice_fusion.1
  3.0 0.7 constant_dynamic-update-slice_fusion.params_ref
  3.7 0.0 copy-start.5
  3.7 0.6 copy-done.5
  4.4 2.2 %shard_map.145 = bf16[16,24,640]{2,1,0:T(8,128)(2,1)} custom-call(s32[1]{0:T(128)} %bitcast.3.view_ref, bf16[6,24,128]{2,1,0:T(8,128)(2,1)} %copy-done.5, bf16[24,128,128]{2,1,0:T(8,128)(2,1)} %feats_ref.1), custom_call_target="tpu_custom_call" | custom-call | tf_op jit(solution)/shard_map/pallas_call | solution.py:399
  6.6 15.7 %all-to-all-start = ((bf16[16,24,640]{2,1,0:T(8,128)(2,1)}), bf16[16,24,640]{2,1,0:T(8,128)(2,1)S(1)}, u32[]{:S(2)}, u32[]{:S(2)}) async-start(bf16[16,24,640]{2,1,0:T(8,128)(2,1)} %shard_map.145), calls=%async_computation | async-start | bytes 983040 | tf_op jit(solution)/shard_map/all_to_all | solution.py:393
  22.3 0.0 copy-done.6
  22.3 0.0 copy-start.1
  22.3 0.0 copy-start.2
  22.3 0.0 copy-start.3
  22.3 0.1 reshape.113
  22.4 0.1 reshape.112
  22.5 0.0 copy-done
  22.5 0.7 gather_fusion
  23.2 22.6 %all-gather = s32[32,1,16]{2,1,0:T(1,128)S(1)} all-gather(s32[1,1,16]{2,1,0:T(1,128)S(1)} %fusion.1), channel_id=1, replica_groups=mesh['view'=32,'tile'=16] {'view'}, dimensions={0}, use_global_device_ids=true | all-gather | bytes 2112 | tf_op jit(solution)/shard_map/all_gather | solution.py:408
  45.8 0.5 broadcast.76
  46.4 0.7 reduce.3
  47.1 0.7 reshape.114.ids_ref
  47.7 0.0 all-to-all-done
  47.7 0.0 copy-start.4
  47.7 0.8 copy-done.4
  48.5 1.6 shard_map.146
  50.1 23.5 %all_to_all.41 = bf16[32,16,640]{2,1,0:T(8,128)(2,1)S(1)} all-to-all(bf16[32,16,640]{2,1,0:T(8,128)(2,1)S(1)} %bitcast.36), channel_id=1, replica_groups=mesh['view'=32,'tile'=16] {'view'}, dimensions={0} | all-to-all | bytes 1310720 | tf_op jit(solution)/shard_map/all_to_all | solution.py:393
  73.6 0.0 copy-done.1
  73.6 0.0 copy-done.2
  73.6 0.0 copy-done.3
  73.6 17.8 %shard_map.147 = (bf16[1,2,1024,128]{3,2,1,0:T(8,128)(2,1)}, bf16[512,640]{1,0:T(8,128)(2,1)S(1)}) custom-call(s32[1,2]{1,0:T(1,128)S(1)} %copy-done.2, f32[1,2]{1,0:T(1,128)S(1)} %copy-done.3, bf16[512,640]{1,0:T(8,128)(2,1)S(1)} %bitcast.35, bf16[1,2,1024,128]{3,2,1,0:T(8,128)(2,1)S(1)} %copy-done.1), custom_call_target="tpu_custom_call" | custom-call | tf_op jit(solution)/shard_map/pallas_call | solution.py:345
  91.4 16.8 %all_to_all.42 = bf16[32,16,640]{2,1,0:T(8,128)(2,1)} all-to-all(bf16[32,16,640]{2,1,0:T(8,128)(2,1)S(1)} %bitcast.38), channel_id=1, replica_groups=mesh['view'=32,'tile'=16] {'view'}, dimensions={0} | all-to-all | bytes 1310720 | tf_op jit(solution)/shard_map/all_to_all | solution.py:393
  108.2 1.7 %shard_map.148 = bf16[384,640]{1,0:T(8,128)(2,1)S(1)} custom-call(s32[1,512]{1,0:T(1,128)} %reshape.114.ids_ref, bf16[512,640]{1,0:T(8,128)(2,1)} %bitcast.39), custom_call_target="tpu_custom_call" | custom-call | tf_op jit(solution)/shard_map/pallas_call | solution.py:335
  109.9 28.0 %all_to_all.43.parts_ref = bf16[16,24,640]{2,1,0:T(8,128)(2,1)} all-to-all(bf16[16,24,640]{2,1,0:T(8,128)(2,1)S(1)} %bitcast.37), channel_id=1, replica_groups=mesh['view'=32,'tile'=16] {'tile'}, dimensions={0} | all-to-all | bytes 983040 | tf_op jit(solution)/shard_map/all_to_all | solution.py:393
  137.9 1.2 shard_map.149
  139.2 27.1 %all_to_all.44.slab_ref = bf16[32,24,640]{2,1,0:T(8,128)(2,1)} all-to-all(bf16[32,24,640]{2,1,0:T(8,128)(2,1)S(1)} %shard_map.149), channel_id=1, replica_groups=mesh['view'=32,'tile'=16] {'view'}, dimensions={0} | all-to-all | bytes 1966080 | tf_op jit(solution)/shard_map/all_to_all | solution.py:393
  166.3 3.0 %shard_map.150 = (f32[24,2,128]{2,1,0:T(2,128)}, f32[24,2,128]{2,1,0:T(2,128)}, f32[24,128]{1,0:T(8,128)}, f32[24,128]{1,0:T(8,128)}, f32[24,128,128]{2,1,0:T(8,128)}) custom-call(bf16[32,24,640]{2,1,0:T(8,128)(2,1)} %all_to_all.44.slab_ref), custom_call_target="tpu_custom_call" | custom-call | tf_op jit(solution)/shard_map/pallas_call | solution.py:423
  (7 shorter events, 0.1 us)
Async XLA Ops:
  0.6 21.9 %copy-start = (s32[384]{0:T(512)S(1)}, s32[384]{0:T(512)}, u32[]{:S(2)}) copy-start(s32[384]{0:T(512)} %param.18) | copy-start | bytes 4612
  0.6 21.7 %copy-start.6 = (s32[1,2,8]{2,1,0:T(2,128)S(1)}, s32[1,2,8]{2,1,0:T(2,128)}, u32[]{:S(2)}) copy-start(s32[1,2,8]{2,1,0:T(2,128)} %param.16) | copy-start | bytes 196
  3.7 0.6 copy-start.5
  6.6 41.2 %all-to-all-start = ((bf16[16,24,640]{2,1,0:T(8,128)(2,1)}), bf16[16,24,640]{2,1,0:T(8,128)(2,1)S(1)}, u32[]{:S(2)}, u32[]{:S(2)}) async-start(bf16[16,24,640]{2,1,0:T(8,128)(2,1)} %shard_map.145), calls=%async_computation | async-start | bytes 983040 | tf_op jit(solution)/shard_map/all_to_all | solution.py:393
  22.3 51.3 %copy-start.1 = (bf16[1,2,1024,128]{3,2,1,0:T(8,128)(2,1)S(1)}, bf16[1,2,1024,128]{3,2,1,0:T(8,128)(2,1)}, u32[]{:S(2)}) copy-start(bf16[1,2,1024,128]{3,2,1,0:T(8,128)(2,1)} %grad_ref.1) | copy-start | bytes 1572868
  22.3 51.3 %copy-start.2 = (s32[1,2]{1,0:T(1,128)S(1)}, s32[1,2]{1,0:T(1,128)}, u32[]{:S(2)}) copy-start(s32[1,2]{1,0:T(1,128)} %pads_ref.1) | copy-start | bytes 28
  22.3 51.3 %copy-start.3 = (f32[1,2]{1,0:T(1,128)S(1)}, f32[1,2]{1,0:T(1,128)}, u32[]{:S(2)}) copy-start(f32[1,2]{1,0:T(1,128)} %offset_ref.1) | copy-start | bytes 28
  47.7 0.8 copy-start.4

commit v3 on v2

--- a/solution.py
+++ b/solution.py
@@ -17,7 +17,7 @@
 WIDTH = 640
 LOG2E = 1.4426950408889634
 CHUNKS = PIX // LANES
-UNROLL = 2
+UNROLL = 8
 f32 = jnp.float32
 bf16 = jnp.bfloat16
 
@@ -309,7 +309,7 @@
         opac_ref[n : n + 1, :] = own[5:6]
 
 
-def cut_kernel(view_ref, params_ref, feats_ref, out_ref):
+def cut_kernel(view_ref, centers_ref, scales_ref, corr_ref, opac_ref, feats_ref, out_ref, pairs):
     held = feats_ref.shape[0]
     view = view_ref[0]
     part = 4
@@ -320,11 +320,21 @@
     for i in range(part):
         hot = jnp.where(column == row * 16 + (view % 4) * part + i, 1.0, 0.0).astype(bf16)
         cuts.append(dot(hot, near))
+    for n in range(held):
+        pairs[0, 2 * n : 2 * n + 2, :] = centers_ref[n].astype(f32)
+        pairs[1, 2 * n : 2 * n + 2, :] = scales_ref[n].astype(f32)
+    row, column = iota((held, 2 * held), 0), iota((held, 2 * held), 1)
+    params = []
+    for which in range(2):
+        for j in range(2):
+            hot = jnp.where(column == 2 * row + j, 1.0, 0.0).astype(bf16)
+            params.append(dot(hot, pairs[which].astype(bf16)).astype(bf16))
+    params += [corr_ref[...], opac_ref[...]]
     gauss, lane = iota((BLOCK, LANES), 0) - view * part, iota((BLOCK, LANES), 1)
     small = jnp.zeros((held, LANES), f32)
-    for j in range(params_ref.shape[0]):
+    for j, param in enumerate(params):
         chosen = (lane == gauss + part * j) & (gauss >= 0) & (gauss < part)
-        small = small + dot(params_ref[j], jnp.where(chosen, 1.0, 0.0).astype(bf16))
+        small = small + dot(param, jnp.where(chosen, 1.0, 0.0).astype(bf16))
     slab = jnp.concatenate(cuts + [small], axis=1).astype(bf16)
     for n in range(out_ref.shape[0]):
         out_ref[n] = slab
@@ -332,6 +342,7 @@
 
 def in_vmem(kernel, shape, *args):
     spec = pl.BlockSpec(memory_space=pltpu.VMEM)
+    args = [pltpu.with_memory_space_constraint(arg, pltpu.VMEM) for arg in args]
     return pl.pallas_call(
         kernel, out_shape=pltpu.VMEM(shape, bf16), in_specs=[spec] * len(args), out_specs=spec
     )(*args)
@@ -392,16 +403,14 @@
     def exchange(x, axis):
         return lax.all_to_all(x, axis, split_axis=0, concat_axis=0, tiled=True)
 
-    params = jnp.stack(
-        [centers[:, 0], centers[:, 1], log_scales[:, 0], log_scales[:, 1], correlation, opacity_logit]
-    )
     spec = pl.BlockSpec(memory_space=pltpu.VMEM)
     slab = pl.pallas_call(
         cut_kernel,
-        out_shape=jax.ShapeDtypeStruct((tiles, held, WIDTH), bf16),
-        in_specs=[pl.BlockSpec(memory_space=pltpu.SMEM), spec, spec],
+        out_shape=pltpu.VMEM((tiles, held, WIDTH), bf16),
+        in_specs=[pl.BlockSpec(memory_space=pltpu.SMEM)] + [spec] * 5,
         out_specs=spec,
-    )(view.reshape(1), params, features)
+        scratch_shapes=[pltpu.VMEM((2, 2 * held, LANES), f32)],
+    )(view.reshape(1), centers, log_scales, correlation, opacity_logit, features)
     table = exchange(slab, "tile")
     rows = jnp.take(block_home, block_list.reshape(-1))
     slots = rows.shape[0]
@@ -432,7 +441,7 @@
             pltpu.VMEM((5, views * held, LANES), f32),
             pltpu.VMEM((held * BLOCK, LANES), f32),
         ],
-    )(slab)
+    )(pltpu.with_memory_space_constraint(slab, pltpu.VMEM))
     return (image, *grads)
 
 

time: 170 us -> 155 us (0.912)
  Pallas kernels: 27.6 us -> 19.3 us
  local copies, waits for them, and re-layouts: 6.48 us -> 1.45 us
    pallas_call x1, Pallas kernels: 17.8 us -> 13.6 us  [tile_call(): pl.pallas_call(tile_kernel, grid=(2,), out_shape=(jax.ShapeDtypeStruct(gr...]
    pallas_call x3, Pallas kernels: 4.59 us -> 1.41 us  [in_vmem(): pl.pallas_call(kernel, out_shape=pltpu.VMEM(shape, bf16), in_specs=[spec]...]
    unnamed x19 -> x10, local copies, waits for them, and re-layouts: 2.16 us -> 0.03 us
  transfers between devices with their start and end apart: 1 -> 1, of which waited for: 0 -> 0; matrix products, arithmetic and copies ran while one was open for 2% -> 1% of each run, Pallas kernels for 0% -> 0%
where the time goes in v3:
time: 155 us
  blocking collectives  117 us (75%)
  Pallas kernels  19.3 us (12%)
  starting transfers between devices  15.7 us (10%)
    all_to_all x4, blocking collectives, exchange(): return lax.all_to_all(x, axis, split_axis=0, concat_axis=0, tiled=True)  94.5 us
    all_gather x1, blocking collectives, shards(): asked = lax.all_gather(rows, 'view')  22.6 us
    all_to_all x1, starting transfers between devices, exchange(): return lax.all_to_all(x, axis, split_axis=0, concat_axis=0, tiled=True)  15.7 us
    pallas_call x1, Pallas kernels, tile_call(): pl.pallas_call(tile_kernel, grid=(2,), out_shape=(jax.ShapeDtypeStruct(gr...  13.6 us
  transfers between devices with their start and end apart: 1, of which 0 were waited for; matrix products, arithmetic and copies ran while one was open for 1% of the time, Pallas kernels for 0%

profile of v3, /device:TPU:1, one launch (start us, length us, event | category | flops | bytes accessed | tf_op | source)
XLA Modules:
  0.0 155.1 jit_solution(649349544965079995)
XLA Ops:
  0.6 0.0 copy-start
  0.6 0.0 copy-start.4
  0.7 2.5 %shard_map.145 = bf16[16,24,640]{2,1,0:T(8,128)(2,1)} custom-call(s32[1]{0:T(128)} %bitcast.3.view_ref, bf16[24,2,128]{2,1,0:T(2,128)(2,1)} %centers_ref.1, bf16[24,2,128]{2,1,0:T(2,128)(2,1)} %scales_ref.1, bf16[24,128]{1,0:T(8,128)(2,1)} %corr_ref.1, bf16[24,128]{1,0:T(8,128)(2,1)} %opac_ref.1, bf16[24,128,128]{2,1,0:T(8,128)(2,1)} %feats_ref.1), custom_call_target="tpu_custom_call" | custom-call | tf_op jit(solution)/shard_map/pallas_call | solution.py:407
  3.1 15.7 %all-to-all-start = ((bf16[16,24,640]{2,1,0:T(8,128)(2,1)}), bf16[16,24,640]{2,1,0:T(8,128)(2,1)S(1)}, u32[]{:S(2)}, u32[]{:S(2)}) async-start(bf16[16,24,640]{2,1,0:T(8,128)(2,1)} %shard_map.145), calls=%async_computation | async-start | bytes 983040 | tf_op jit(solution)/shard_map/all_to_all | solution.py:404
  18.9 0.0 copy-done.4
  18.9 0.0 copy-start.1
  18.9 0.0 copy-start.2
  18.9 0.0 copy-start.3
  18.9 0.1 reshape.113
  19.0 0.1 reshape.112
  19.1 0.0 copy-done
  19.1 0.7 gather_fusion
  19.8 22.6 %all-gather = s32[32,1,16]{2,1,0:T(1,128)S(1)} all-gather(s32[1,1,16]{2,1,0:T(1,128)S(1)} %fusion.1), channel_id=1, replica_groups=mesh['view'=32,'tile'=16] {'view'}, dimensions={0}, use_global_device_ids=true | all-gather | bytes 2112 | tf_op jit(solution)/shard_map/all_gather | solution.py:417
  42.4 0.5 broadcast.76
  42.9 0.7 reduce.3
  43.6 0.1 reshape.114.ids_ref
  43.7 0.0 all-to-all-done
  43.7 0.6 shard_map.146
  44.3 24.0 %all_to_all.41 = bf16[32,16,640]{2,1,0:T(8,128)(2,1)S(1)} all-to-all(bf16[32,16,640]{2,1,0:T(8,128)(2,1)S(1)} %bitcast.17), channel_id=1, replica_groups=mesh['view'=32,'tile'=16] {'view'}, dimensions={0} | all-to-all | bytes 1310720 | tf_op jit(solution)/shard_map/all_to_all | solution.py:404
  68.3 0.0 copy-done.1
  68.3 0.0 copy-done.2
  68.4 0.0 copy-done.3
  68.4 13.6 %shard_map.147 = (bf16[1,2,1024,128]{3,2,1,0:T(8,128)(2,1)}, bf16[512,640]{1,0:T(8,128)(2,1)S(1)}) custom-call(s32[1,2]{1,0:T(1,128)S(1)} %copy-done.2, f32[1,2]{1,0:T(1,128)S(1)} %copy-done.3, bf16[512,640]{1,0:T(8,128)(2,1)S(1)} %bitcast.15, bf16[1,2,1024,128]{3,2,1,0:T(8,128)(2,1)S(1)} %copy-done.1), custom_call_target="tpu_custom_call" | custom-call | tf_op jit(solution)/shard_map/pallas_call | solution.py:356
  82.0 16.4 %all_to_all.42 = bf16[32,16,640]{2,1,0:T(8,128)(2,1)S(1)} all-to-all(bf16[32,16,640]{2,1,0:T(8,128)(2,1)S(1)} %bitcast.20), channel_id=1, replica_groups=mesh['view'=32,'tile'=16] {'view'}, dimensions={0} | all-to-all | bytes 1310720 | tf_op jit(solution)/shard_map/all_to_all | solution.py:404
  98.4 0.6 shard_map.148
  99.0 27.3 %all_to_all.43.parts_ref = bf16[16,24,640]{2,1,0:T(8,128)(2,1)S(1)} all-to-all(bf16[16,24,640]{2,1,0:T(8,128)(2,1)S(1)} %bitcast.19), channel_id=1, replica_groups=mesh['view'=32,'tile'=16] {'tile'}, dimensions={0} | all-to-all | bytes 983040 | tf_op jit(solution)/shard_map/all_to_all | solution.py:404
  126.4 0.2 shard_map.149
  126.6 26.7 %all_to_all.44.slab_ref = bf16[32,24,640]{2,1,0:T(8,128)(2,1)S(1)} all-to-all(bf16[32,24,640]{2,1,0:T(8,128)(2,1)S(1)} %shard_map.149), channel_id=1, replica_groups=mesh['view'=32,'tile'=16] {'view'}, dimensions={0} | all-to-all | bytes 1966080 | tf_op jit(solution)/shard_map/all_to_all | solution.py:404
  153.3 1.8 %shard_map.150 = (f32[24,2,128]{2,1,0:T(2,128)}, f32[24,2,128]{2,1,0:T(2,128)}, f32[24,128]{1,0:T(8,128)}, f32[24,128]{1,0:T(8,128)}, f32[24,128,128]{2,1,0:T(8,128)}) custom-call(bf16[32,24,640]{2,1,0:T(8,128)(2,1)S(1)} %all_to_all.44.slab_ref), custom_call_target="tpu_custom_call" | custom-call | tf_op jit(solution)/shard_map/pallas_call | solution.py:432
  (3 shorter events, 0.0 us)
Async XLA Ops:
  0.6 18.5 %copy-start = (s32[384]{0:T(512)S(1)}, s32[384]{0:T(512)}, u32[]{:S(2)}) copy-start(s32[384]{0:T(512)} %param.18) | copy-start | bytes 4612
  0.6 18.2 %copy-start.4 = (s32[1,2,8]{2,1,0:T(2,128)S(1)}, s32[1,2,8]{2,1,0:T(2,128)}, u32[]{:S(2)}) copy-start(s32[1,2,8]{2,1,0:T(2,128)} %param.16) | copy-start | bytes 196
  3.1 40.6 %all-to-all-start = ((bf16[16,24,640]{2,1,0:T(8,128)(2,1)}), bf16[16,24,640]{2,1,0:T(8,128)(2,1)S(1)}, u32[]{:S(2)}, u32[]{:S(2)}) async-start(bf16[16,24,640]{2,1,0:T(8,128)(2,1)} %shard_map.145), calls=%async_computation | async-start | bytes 983040 | tf_op jit(solution)/shard_map/all_to_all | solution.py:404
  18.9 49.5 %copy-start.1 = (bf16[1,2,1024,128]{3,2,1,0:T(8,128)(2,1)S(1)}, bf16[1,2,1024,128]{3,2,1,0:T(8,128)(2,1)}, u32[]{:S(2)}) copy-start(bf16[1,2,1024,128]{3,2,1,0:T(8,128)(2,1)} %grad_ref.1) | copy-start | bytes 1572868
  18.9 49.5 %copy-start.2 = (s32[1,2]{1,0:T(1,128)S(1)}, s32[1,2]{1,0:T(1,128)}, u32[]{:S(2)}) copy-start(s32[1,2]{1,0:T(1,128)} %pads_ref.1) | copy-start | bytes 28
  18.9 49.5 %copy-start.3 = (f32[1,2]{1,0:T(1,128)S(1)}, f32[1,2]{1,0:T(1,128)}, u32[]{:S(2)}) copy-start(f32[1,2]{1,0:T(1,128)} %offset_ref.1) | copy-start | bytes 28

commit v4 on v3

--- a/solution.py
+++ b/solution.py
@@ -15,6 +15,8 @@
 LIST = 8
 LANES = 128
 WIDTH = 640
+HELD = 24
+SENT = 4 * HELD + 8
 LOG2E = 1.4426950408889634
 CHUNKS = PIX // LANES
 UNROLL = 8
@@ -38,38 +40,73 @@
     return pltpu.roll(x, shift % LANES, 1)
 
 
-def split_pairs(x):
-    kept = jnp.where(iota(x.shape, 1) < 32, x, 0.0)
-    high = kept.astype(bf16).astype(f32)
-    return high + lane_roll(kept - high, 32)
-
-
 def fold_pairs(x):
     return x + lane_roll(x, -32)
 
 
-def gather_kernel(ids_ref, table_ref, out_ref):
-    rows = table_ref.shape[0]
-    count = ids_ref.shape[1]
-    hot = jnp.where(iota((rows, count), 0) == ids_ref[...], 1.0, 0.0).astype(bf16)
-    out_ref[...] = dot(hot, table_ref[...], TN).astype(bf16)
+def one_hot(mask):
+    return jnp.where(mask, 1.0, 0.0).astype(bf16)
+
+
+def pack_rows(x):
+    shards_here = x.shape[0] // HELD
+    row, column = iota((8 * shards_here, x.shape[0]), 0), iota((8 * shards_here, x.shape[0]), 1)
+    out = jnp.zeros((8 * shards_here, LANES), f32)
+    for q in range(4):
+        hot = one_hot((column == (row // 8) * HELD + 6 * q + row % 8) & (row % 8 < 6))
+        out = out + lane_roll(dot(hot, x), 32 * q)
+    return out
+
+
+def unpack_rows(x):
+    shards_here = x.shape[0] // 8
+    row, column = iota((HELD * shards_here, x.shape[0]), 0), iota((HELD * shards_here, x.shape[0]), 1)
+    out = jnp.zeros((HELD * shards_here, LANES), f32)
+    for q in range(4):
+        hot = one_hot((row == (column // 8) * HELD + 6 * q + column % 8) & (column % 8 < 6))
+        piece = jnp.where(iota(x.shape, 1) < 32, lane_roll(x, -32 * q), 0.0)
+        out = out + dot(hot, piece.astype(bf16))
+    return out
+
+
+def gather_kernel(ids_ref, table_ref, out_ref, wide):
+    tiles = table_ref.shape[0]
+    rows, count = tiles * HELD, ids_ref.shape[1]
+    for z in range(tiles):
+        for i in range(4):
+            wide[HELD * z : HELD * (z + 1), F * i : F * (i + 1)] = table_ref[
+                z, HELD * i : HELD * (i + 1), :
+            ].astype(f32)
+    small = [table_ref[z, 4 * HELD :, :].astype(f32) for z in range(tiles)]
+    wide[:, 4 * F :] = unpack_rows(jnp.concatenate(small, axis=0))
+    hot = one_hot(iota((rows, count), 0) == ids_ref[...])
+    out_ref[...] = dot(hot, wide[...].astype(bf16), TN).astype(bf16)
 
 
 def scatter_kernel(ids_ref, grads_ref, out_ref):
-    rows = out_ref.shape[0]
-    count = ids_ref.shape[1]
-    hot = jnp.where(iota((rows, count), 0) == ids_ref[...], 1.0, 0.0).astype(bf16)
+    tiles = out_ref.shape[0]
+    rows, count = tiles * HELD, ids_ref.shape[1]
+    hot = one_hot(iota((rows, count), 0) == ids_ref[...])
     total = dot(hot, grads_ref[...])
-    out_ref[:, : 4 * F] = total[:, : 4 * F].astype(bf16)
-    out_ref[:, 4 * F :] = split_pairs(fold_pairs(total[:, 4 * F :])).astype(bf16)
+    small = fold_pairs(total[:, 4 * F :])
+    small = pack_rows(jnp.where(iota(small.shape, 1) < 32, small, 0.0).astype(bf16))
+    for z in range(tiles):
+        for i in range(4):
+            out_ref[z, HELD * i : HELD * (i + 1), :] = total[
+                HELD * z : HELD * (z + 1), F * i : F * (i + 1)
+            ].astype(bf16)
+        out_ref[z, 4 * HELD :, :] = small[8 * z : 8 * z + 8].astype(bf16)
 
 
 def sum_kernel(parts_ref, out_ref):
     total = parts_ref[0].astype(f32)
     for n in range(1, parts_ref.shape[0]):
         total = total + parts_ref[n].astype(f32)
-    pairs = split_pairs(fold_pairs(total[:, 4 * F :]))
-    total = jnp.concatenate([total[:, : 4 * F], pairs], axis=1).astype(bf16)
+    small = total[4 * HELD :]
+    high = small.astype(bf16).astype(f32)
+    pairs = unpack_rows(high) + lane_roll(unpack_rows(small - high), 32)
+    parts = [total[HELD * i : HELD * (i + 1)] for i in range(4)] + [pairs]
+    total = jnp.concatenate(parts, axis=1).astype(bf16)
     for n in range(out_ref.shape[0]):
         out_ref[n] = total
 
@@ -335,16 +372,20 @@
     for j, param in enumerate(params):
         chosen = (lane == gauss + part * j) & (gauss >= 0) & (gauss < part)
         small = small + dot(param, jnp.where(chosen, 1.0, 0.0).astype(bf16))
-    slab = jnp.concatenate(cuts + [small], axis=1).astype(bf16)
+    slab = jnp.concatenate(cuts + [pack_rows(small.astype(bf16))], axis=0).astype(bf16)
     for n in range(out_ref.shape[0]):
         out_ref[n] = slab
 
 
-def in_vmem(kernel, shape, *args):
+def in_vmem(kernel, shape, *args, scratch=()):
     spec = pl.BlockSpec(memory_space=pltpu.VMEM)
     args = [pltpu.with_memory_space_constraint(arg, pltpu.VMEM) for arg in args]
     return pl.pallas_call(
-        kernel, out_shape=pltpu.VMEM(shape, bf16), in_specs=[spec] * len(args), out_specs=spec
+        kernel,
+        out_shape=pltpu.VMEM(shape, bf16),
+        in_specs=[spec] * len(args),
+        out_specs=spec,
+        scratch_shapes=scratch,
     )(*args)
 
 
@@ -406,7 +447,7 @@
     spec = pl.BlockSpec(memory_space=pltpu.VMEM)
     slab = pl.pallas_call(
         cut_kernel,
-        out_shape=pltpu.VMEM((tiles, held, WIDTH), bf16),
+        out_shape=pltpu.VMEM((tiles, SENT, LANES), bf16),
         in_specs=[pl.BlockSpec(memory_space=pltpu.SMEM)] + [spec] * 5,
         out_specs=spec,
         scratch_shapes=[pltpu.VMEM((2, 2 * held, LANES), f32)],
@@ -415,15 +456,18 @@
     rows = jnp.take(block_home, block_list.reshape(-1))
     slots = rows.shape[0]
     asked = lax.all_gather(rows, "view")
-    table, ids = table.reshape(total, WIDTH), asked.reshape(1, -1)
-    wanted = in_vmem(gather_kernel, (views * slots, WIDTH), ids, table)
+    ids = asked.reshape(1, -1)
+    wanted = in_vmem(
+        gather_kernel, (views * slots, WIDTH), ids, table,
+        scratch=[pltpu.VMEM((total, WIDTH), f32)],
+    )
     blocks = exchange(wanted, "view")
 
     image, sent = tile_call(pad_count, view_offset, blocks, image_grad)
 
     came = exchange(sent, "view")
-    partial = in_vmem(scatter_kernel, (total, WIDTH), ids, came)
-    partial = exchange(partial, "tile").reshape(tiles, held, WIDTH)
+    partial = in_vmem(scatter_kernel, (tiles, SENT, LANES), ids, came)
+    partial = exchange(partial, "tile")
     slab = in_vmem(sum_kernel, (views, held, WIDTH), partial)
     slab = exchange(slab, "view")
 

time: 155 us -> 154 us (level)
  blocking collectives: 117 us -> 115 us
    all_to_all x4, blocking collectives: 94.5 us -> 92 us  [exchange(): return lax.all_to_all(x, axis, split_axis=0, concat_axis=0, tiled=True)]
where the time goes in v4:
time: 154 us; the launch traced here: 153 us
  blocking collectives  115 us (75%)
  Pallas kernels  20.1 us (13%)
  starting transfers between devices  15.7 us (10%)
    all_to_all x4, blocking collectives, exchange(): return lax.all_to_all(x, axis, split_axis=0, concat_axis=0, tiled=True)  92 us
    all_gather x1, blocking collectives, shards(): asked = lax.all_gather(rows, 'view')  22.6 us
    all_to_all x1, starting transfers between devices, exchange(): return lax.all_to_all(x, axis, split_axis=0, concat_axis=0, tiled=True)  15.7 us
    pallas_call x1, Pallas kernels, tile_call(): pl.pallas_call(tile_kernel, grid=(2,), out_shape=(jax.ShapeDtypeStruct(gr...  13.6 us
  transfers between devices with their start and end apart: 1, of which 0 were waited for; matrix products, arithmetic and copies ran while one was open for 1% of the time, Pallas kernels for 0%

profile of v4, /device:TPU:1, one launch (start us, length us, event | category | flops | bytes accessed | tf_op | source)
XLA Modules:
  0.0 153.4 jit_solution(296783280398631667)
XLA Ops:
  0.6 0.0 copy-start
  0.6 0.0 copy-start.4
  0.7 2.6 %shard_map.145 = bf16[16,104,128]{2,1,0:T(8,128)(2,1)} custom-call(s32[1]{0:T(128)} %bitcast.3.view_ref, bf16[24,2,128]{2,1,0:T(2,128)(2,1)} %centers_ref.1, bf16[24,2,128]{2,1,0:T(2,128)(2,1)} %scales_ref.1, bf16[24,128]{1,0:T(8,128)(2,1)} %corr_ref.1, bf16[24,128]{1,0:T(8,128)(2,1)} %opac_ref.1, bf16[24,128,128]{2,1,0:T(8,128)(2,1)} %feats_ref.1), custom_call_target="tpu_custom_call" | custom-call | tf_op jit(solution)/shard_map/pallas_call | solution.py:448
  3.3 15.7 %all-to-all-start = ((bf16[16,104,128]{2,1,0:T(8,128)(2,1)}), bf16[16,104,128]{2,1,0:T(8,128)(2,1)S(1)}, u32[]{:S(2)}, u32[]{:S(2)}) async-start(bf16[16,104,128]{2,1,0:T(8,128)(2,1)} %shard_map.145), calls=%async_computation | async-start | bytes 851968 | tf_op jit(solution)/shard_map/all_to_all | solution.py:445
  19.0 0.0 copy-done.4
  19.0 0.0 copy-start.1
  19.0 0.0 copy-start.2
  19.1 0.0 copy-start.3
  19.1 0.1 reshape.106
  19.1 0.1 reshape.105
  19.2 0.0 copy-done
  19.2 0.7 gather_fusion
  19.9 22.6 %all-gather = s32[32,1,16]{2,1,0:T(1,128)S(1)} all-gather(s32[1,1,16]{2,1,0:T(1,128)S(1)} %fusion.1), channel_id=1, replica_groups=mesh['view'=32,'tile'=16] {'view'}, dimensions={0}, use_global_device_ids=true | all-gather | bytes 2112 | tf_op jit(solution)/shard_map/all_gather | solution.py:458
  42.6 0.5 broadcast.76
  43.1 0.7 reduce.3
  43.8 0.1 reshape.107.ids_ref
  43.8 0.0 all-to-all-done.table_ref
  43.8 0.7 shard_map.146
  44.6 21.0 %all_to_all.37 = bf16[32,16,640]{2,1,0:T(8,128)(2,1)S(1)} all-to-all(bf16[32,16,640]{2,1,0:T(8,128)(2,1)S(1)} %bitcast.15), channel_id=1, replica_groups=mesh['view'=32,'tile'=16] {'view'}, dimensions={0} | all-to-all | bytes 1310720 | tf_op jit(solution)/shard_map/all_to_all | solution.py:445
  65.6 0.0 copy-done.1
  65.6 0.0 copy-done.2
  65.6 0.0 copy-done.3
  65.6 13.6 %shard_map.147 = (bf16[1,2,1024,128]{3,2,1,0:T(8,128)(2,1)}, bf16[512,640]{1,0:T(8,128)(2,1)S(1)}) custom-call(s32[1,2]{1,0:T(1,128)S(1)} %copy-done.2, f32[1,2]{1,0:T(1,128)S(1)} %copy-done.3, bf16[512,640]{1,0:T(8,128)(2,1)S(1)} %bitcast.13, bf16[1,2,1024,128]{3,2,1,0:T(8,128)(2,1)S(1)} %copy-done.1), custom_call_target="tpu_custom_call" | custom-call | tf_op jit(solution)/shard_map/pallas_call | solution.py:397
  79.2 16.4 %all_to_all.38 = bf16[32,16,640]{2,1,0:T(8,128)(2,1)S(1)} all-to-all(bf16[32,16,640]{2,1,0:T(8,128)(2,1)S(1)} %bitcast.16), channel_id=1, replica_groups=mesh['view'=32,'tile'=16] {'view'}, dimensions={0} | all-to-all | bytes 1310720 | tf_op jit(solution)/shard_map/all_to_all | solution.py:445
  95.6 1.0 shard_map.148
  96.6 28.5 %all_to_all.39.parts_ref = bf16[16,104,128]{2,1,0:T(8,128)(2,1)S(1)} all-to-all(bf16[16,104,128]{2,1,0:T(8,128)(2,1)S(1)} %shard_map.148), channel_id=1, replica_groups=mesh['view'=32,'tile'=16] {'tile'}, dimensions={0} | all-to-all | bytes 851968 | tf_op jit(solution)/shard_map/all_to_all | solution.py:445
  125.1 0.3 shard_map.149
  125.4 26.1 %all_to_all.40.slab_ref = bf16[32,24,640]{2,1,0:T(8,128)(2,1)S(1)} all-to-all(bf16[32,24,640]{2,1,0:T(8,128)(2,1)S(1)} %shard_map.149), channel_id=1, replica_groups=mesh['view'=32,'tile'=16] {'view'}, dimensions={0} | all-to-all | bytes 1966080 | tf_op jit(solution)/shard_map/all_to_all | solution.py:445
  151.6 1.8 %shard_map.150 = (f32[24,2,128]{2,1,0:T(2,128)}, f32[24,2,128]{2,1,0:T(2,128)}, f32[24,128]{1,0:T(8,128)}, f32[24,128]{1,0:T(8,128)}, f32[24,128,128]{2,1,0:T(8,128)}) custom-call(bf16[32,24,640]{2,1,0:T(8,128)(2,1)S(1)} %all_to_all.40.slab_ref), custom_call_target="tpu_custom_call" | custom-call | tf_op jit(solution)/shard_map/pallas_call | solution.py:476
  (3 shorter events, 0.0 us)
Async XLA Ops:
  0.6 18.6 %copy-start = (s32[384]{0:T(512)S(1)}, s32[384]{0:T(512)}, u32[]{:S(2)}) copy-start(s32[384]{0:T(512)} %param.18) | copy-start | bytes 4612
  0.6 18.4 %copy-start.4 = (s32[1,2,8]{2,1,0:T(2,128)S(1)}, s32[1,2,8]{2,1,0:T(2,128)}, u32[]{:S(2)}) copy-start(s32[1,2,8]{2,1,0:T(2,128)} %param.16) | copy-start | bytes 196
  3.3 40.6 %all-to-all-start = ((bf16[16,104,128]{2,1,0:T(8,128)(2,1)}), bf16[16,104,128]{2,1,0:T(8,128)(2,1)S(1)}, u32[]{:S(2)}, u32[]{:S(2)}) async-start(bf16[16,104,128]{2,1,0:T(8,128)(2,1)} %shard_map.145), calls=%async_computation | async-start | bytes 851968 | tf_op jit(solution)/shard_map/all_to_all | solution.py:445
  19.0 46.5 %copy-start.1 = (bf16[1,2,1024,128]{3,2,1,0:T(8,128)(2,1)S(1)}, bf16[1,2,1024,128]{3,2,1,0:T(8,128)(2,1)}, u32[]{:S(2)}) copy-start(bf16[1,2,1024,128]{3,2,1,0:T(8,128)(2,1)} %grad_ref.1) | copy-start | bytes 1572868
  19.0 46.5 %copy-start.2 = (s32[1,2]{1,0:T(1,128)S(1)}, s32[1,2]{1,0:T(1,128)}, u32[]{:S(2)}) copy-start(s32[1,2]{1,0:T(1,128)} %pads_ref.1) | copy-start | bytes 28
  19.1 46.5 %copy-start.3 = (f32[1,2]{1,0:T(1,128)S(1)}, f32[1,2]{1,0:T(1,128)}, u32[]{:S(2)}) copy-start(f32[1,2]{1,0:T(1,128)} %offset_ref.1) | copy-start | bytes 28

commit v5 on v4

--- a/solution.py
+++ b/solution.py
@@ -69,9 +69,19 @@
     return out
 
 
-def gather_kernel(ids_ref, table_ref, out_ref, wide):
+def gather_kernel(lists_ref, table_ref, out_ref, ids_ref, lists, wide):
     tiles = table_ref.shape[0]
-    rows, count = tiles * HELD, ids_ref.shape[1]
+    views, slots = lists.shape
+    rows, count = tiles * HELD, views * slots
+    for v in range(views):
+        lists[v : v + 1, :] = lists_ref[v]
+    ids = lists[...]
+    hot = one_hot(iota((slots, count), 1) % slots == iota((slots, count), 0))
+    ids = 16.0 * dot((ids // 16).astype(f32).astype(bf16), hot) + dot(
+        (ids % 16).astype(f32).astype(bf16), hot
+    )
+    ids = jnp.where(iota((views, count), 1) // slots == iota((views, count), 0), ids, 0.0)
+    ids_ref[...] = jnp.sum(ids, axis=0, keepdims=True).astype(jnp.int32)
     for z in range(tiles):
         for i in range(4):
             wide[HELD * z : HELD * (z + 1), F * i : F * (i + 1)] = table_ref[
@@ -102,11 +112,7 @@
     total = parts_ref[0].astype(f32)
     for n in range(1, parts_ref.shape[0]):
         total = total + parts_ref[n].astype(f32)
-    small = total[4 * HELD :]
-    high = small.astype(bf16).astype(f32)
-    pairs = unpack_rows(high) + lane_roll(unpack_rows(small - high), 32)
-    parts = [total[HELD * i : HELD * (i + 1)] for i in range(4)] + [pairs]
-    total = jnp.concatenate(parts, axis=1).astype(bf16)
+    total = total.astype(bf16)
     for n in range(out_ref.shape[0]):
         out_ref[n] = total
 
@@ -323,19 +329,23 @@
         sent_ref[...] = dot(perm[...], back[...], TN).astype(bf16)
 
 
-def finish_kernel(slab_ref, centers_ref, scales_ref, corr_ref, opac_ref, feats_ref, wide, tall):
-    slices, held = slab_ref.shape[0], slab_ref.shape[1]
+def finish_kernel(slab_ref, centers_ref, scales_ref, corr_ref, opac_ref, feats_ref, wide, small, tall):
+    slices, held = slab_ref.shape[0], HELD
     for n in range(slices):
-        for i in range(5):
-            wide[i, held * n : held * (n + 1), :] = slab_ref[n, :, F * i : F * (i + 1)].astype(f32)
+        for i in range(4):
+            wide[i, held * n : held * (n + 1), :] = slab_ref[
+                n, held * i : held * (i + 1), :
+            ].astype(f32)
+        small[8 * n : 8 * n + 8, :] = slab_ref[n, 4 * held :, :].astype(f32)
     lane = iota((slices, LANES), 1)
-    place = jnp.where(lane < 64, (lane % 32) // 8, -1)
     for n in range(held):
         at = pl.ds(n, slices, stride=held)
-        small = wide[4, at, :]
+        packed = small[pl.ds(n % 6, slices, stride=8), :]
         for i in range(4):
             feats_ref[n, pl.ds(i, slices, stride=4), :] = wide[i, at, :]
-            tall[pl.ds(BLOCK * n + i, slices, stride=4), :] = jnp.where(place == i, small, 0.0)
+            tall[pl.ds(BLOCK * n + i, slices, stride=4), :] = jnp.where(
+                lane // 8 == 4 * (n // 6) + i, packed, 0.0
+            )
     rank = jnp.where(iota((8, LANES), 1) % 8 == iota((8, LANES), 0), 1.0, 0.0).astype(bf16)
     table = dot(rank, tall[...].astype(bf16), NT)
     for n in range(held):
@@ -377,7 +387,7 @@
         out_ref[n] = slab
 
 
-def in_vmem(kernel, shape, *args, scratch=()):
+def in_vmem(kernel, shape, *args):
     spec = pl.BlockSpec(memory_space=pltpu.VMEM)
     args = [pltpu.with_memory_space_constraint(arg, pltpu.VMEM) for arg in args]
     return pl.pallas_call(
@@ -385,7 +395,6 @@
         out_shape=pltpu.VMEM(shape, bf16),
         in_specs=[spec] * len(args),
         out_specs=spec,
-        scratch_shapes=scratch,
     )(*args)
 
 
@@ -455,12 +464,18 @@
     table = exchange(slab, "tile")
     rows = jnp.take(block_home, block_list.reshape(-1))
     slots = rows.shape[0]
-    asked = lax.all_gather(rows, "view")
-    ids = asked.reshape(1, -1)
-    wanted = in_vmem(
-        gather_kernel, (views * slots, WIDTH), ids, table,
-        scratch=[pltpu.VMEM((total, WIDTH), f32)],
-    )
+    asked = lax.all_gather(rows.reshape(1, 1, slots), "view", tiled=True)
+    wanted, ids = pl.pallas_call(
+        gather_kernel,
+        out_shape=(
+            pltpu.VMEM((views * slots, WIDTH), bf16), pltpu.VMEM((1, views * slots), jnp.int32)
+        ),
+        in_specs=[spec] * 2,
+        out_specs=(spec,) * 2,
+        scratch_shapes=[
+            pltpu.VMEM((views, slots), jnp.int32), pltpu.VMEM((total, WIDTH), f32)
+        ],
+    )(*(pltpu.with_memory_space_constraint(x, pltpu.VMEM) for x in (asked, table)))
     blocks = exchange(wanted, "view")
 
     image, sent = tile_call(pad_count, view_offset, blocks, image_grad)
@@ -468,7 +483,7 @@
     came = exchange(sent, "view")
     partial = in_vmem(scatter_kernel, (tiles, SENT, LANES), ids, came)
     partial = exchange(partial, "tile")
-    slab = in_vmem(sum_kernel, (views, held, WIDTH), partial)
+    slab = in_vmem(sum_kernel, (views, SENT, LANES), partial)
     slab = exchange(slab, "view")
 
     shape = lambda *dims: jax.ShapeDtypeStruct(dims, f32)
@@ -482,7 +497,8 @@
         in_specs=[spec],
         out_specs=(spec,) * 5,
         scratch_shapes=[
-            pltpu.VMEM((5, views * held, LANES), f32),
+            pltpu.VMEM((4, views * held, LANES), f32),
+            pltpu.VMEM((views * 8, LANES), f32),
             pltpu.VMEM((held * BLOCK, LANES), f32),
         ],
     )(pltpu.with_memory_space_constraint(slab, pltpu.VMEM))

time: 154 us -> 151 us (0.981)
  blocking collectives: 115 us -> 113 us
where the time goes in v5:
time: 151 us
  blocking collectives  113 us (75%)
  Pallas kernels  20 us (13%)
  starting transfers between devices  15.9 us (11%)
    all_to_all x4, blocking collectives, exchange(): return lax.all_to_all(x, axis, split_axis=0, concat_axis=0, tiled=True)  90.6 us
    all_gather x1, blocking collectives, shards(): asked = lax.all_gather(rows.reshape(1, 1, slots), 'view', tiled=True)  22.6 us
    all_to_all x1, starting transfers between devices, exchange(): return lax.all_to_all(x, axis, split_axis=0, concat_axis=0, tiled=True)  15.9 us
    pallas_call x1, Pallas kernels, tile_call(): pl.pallas_call(tile_kernel, grid=(2,), out_shape=(jax.ShapeDtypeStruct(gr...  13.6 us
  transfers between devices with their start and end apart: 1, of which 0 were waited for; matrix products, arithmetic and copies ran while one was open for 1% of the time, Pallas kernels for 0%

profile of v5, /device:TPU:1, one launch (start us, length us, event | category | flops | bytes accessed | tf_op | source)
XLA Modules:
  0.0 150.7 jit_solution(12414315449745070132)
XLA Ops:
  0.6 0.0 copy-start
  0.6 0.0 copy-start.4
  0.7 2.6 %shard_map.145 = bf16[16,104,128]{2,1,0:T(8,128)(2,1)} custom-call(s32[1]{0:T(128)} %bitcast.2.view_ref, bf16[24,2,128]{2,1,0:T(2,128)(2,1)} %centers_ref.1, bf16[24,2,128]{2,1,0:T(2,128)(2,1)} %scales_ref.1, bf16[24,128]{1,0:T(8,128)(2,1)} %corr_ref.1, bf16[24,128]{1,0:T(8,128)(2,1)} %opac_ref.1, bf16[24,128,128]{2,1,0:T(8,128)(2,1)} %feats_ref.1), custom_call_target="tpu_custom_call" | custom-call | tf_op jit(solution)/shard_map/pallas_call | solution.py:457
  3.3 0.0 copy-start.1
  3.3 0.0 copy-start.2
  3.3 0.0 copy-start.3
  3.3 15.9 %all-to-all-start = ((bf16[16,104,128]{2,1,0:T(8,128)(2,1)}), bf16[16,104,128]{2,1,0:T(8,128)(2,1)S(1)}, u32[]{:S(2)}, u32[]{:S(2)}) async-start(bf16[16,104,128]{2,1,0:T(8,128)(2,1)} %shard_map.145), calls=%async_computation | async-start | bytes 851968 | tf_op jit(solution)/shard_map/all_to_all | solution.py:454
  19.2 0.0 copy-done.4
  19.2 0.1 reshape.104
  19.3 0.1 reshape.103
  19.3 0.0 copy-done
  19.4 0.7 gather_fusion
  20.0 22.6 %all_gather.3.lists_ref = s32[32,1,16]{2,1,0:T(1,128)S(1)} all-gather(s32[1,1,16]{2,1,0:T(1,128)S(1)} %and_select_fusion), channel_id=1, replica_groups=mesh['view'=32,'tile'=16] {'view'}, dimensions={0}, use_global_device_ids=true | all-gather | bytes 2112 | tf_op jit(solution)/shard_map/all_gather | solution.py:467
  42.7 0.0 all-to-all-done.table_ref
  42.7 0.9 shard_map.146
  43.6 22.3 %all_to_all.37 = bf16[32,16,640]{2,1,0:T(8,128)(2,1)S(1)} all-to-all(bf16[32,16,640]{2,1,0:T(8,128)(2,1)S(1)} %bitcast.11), channel_id=1, replica_groups=mesh['view'=32,'tile'=16] {'view'}, dimensions={0} | all-to-all | bytes 1310720 | tf_op jit(solution)/shard_map/all_to_all | solution.py:454
  65.8 0.0 copy-done.1
  65.8 0.0 copy-done.2
  65.9 0.0 copy-done.3
  65.9 13.6 %shard_map.147 = (bf16[1,2,1024,128]{3,2,1,0:T(8,128)(2,1)}, bf16[512,640]{1,0:T(8,128)(2,1)S(1)}) custom-call(s32[1,2]{1,0:T(1,128)S(1)} %copy-done.2, f32[1,2]{1,0:T(1,128)S(1)} %copy-done.3, bf16[512,640]{1,0:T(8,128)(2,1)S(1)} %bitcast.9, bf16[1,2,1024,128]{3,2,1,0:T(8,128)(2,1)S(1)} %copy-done.1), custom_call_target="tpu_custom_call" | custom-call | tf_op jit(solution)/shard_map/pallas_call | solution.py:406
  79.5 16.4 %all_to_all.38 = bf16[32,16,640]{2,1,0:T(8,128)(2,1)S(1)} all-to-all(bf16[32,16,640]{2,1,0:T(8,128)(2,1)S(1)} %bitcast.12), channel_id=1, replica_groups=mesh['view'=32,'tile'=16] {'view'}, dimensions={0} | all-to-all | bytes 1310720 | tf_op jit(solution)/shard_map/all_to_all | solution.py:454
  95.9 1.0 shard_map.148
  96.9 27.1 %all_to_all.39.parts_ref = bf16[16,104,128]{2,1,0:T(8,128)(2,1)S(1)} all-to-all(bf16[16,104,128]{2,1,0:T(8,128)(2,1)S(1)} %shard_map.148), channel_id=1, replica_groups=mesh['view'=32,'tile'=16] {'tile'}, dimensions={0} | all-to-all | bytes 851968 | tf_op jit(solution)/shard_map/all_to_all | solution.py:454
  124.1 0.1 shard_map.149
  124.2 24.7 %all_to_all.40.slab_ref = bf16[32,104,128]{2,1,0:T(8,128)(2,1)S(1)} all-to-all(bf16[32,104,128]{2,1,0:T(8,128)(2,1)S(1)} %shard_map.149), channel_id=1, replica_groups=mesh['view'=32,'tile'=16] {'view'}, dimensions={0} | all-to-all | bytes 1703936 | tf_op jit(solution)/shard_map/all_to_all | solution.py:454
  148.9 1.8 %shard_map.150 = (f32[24,2,128]{2,1,0:T(2,128)}, f32[24,2,128]{2,1,0:T(2,128)}, f32[24,128]{1,0:T(8,128)}, f32[24,128]{1,0:T(8,128)}, f32[24,128,128]{2,1,0:T(8,128)}) custom-call(bf16[32,104,128]{2,1,0:T(8,128)(2,1)S(1)} %all_to_all.40.slab_ref), custom_call_target="tpu_custom_call" | custom-call | tf_op jit(solution)/shard_map/pallas_call | solution.py:491
  (3 shorter events, 0.0 us)
Async XLA Ops:
  0.6 18.7 %copy-start = (s32[384]{0:T(512)S(1)}, s32[384]{0:T(512)}, u32[]{:S(2)}) copy-start(s32[384]{0:T(512)} %param.18) | copy-start | bytes 4612
  0.6 18.5 %copy-start.4 = (s32[1,2,8]{2,1,0:T(2,128)S(1)}, s32[1,2,8]{2,1,0:T(2,128)}, u32[]{:S(2)}) copy-start(s32[1,2,8]{2,1,0:T(2,128)} %param.16) | copy-start | bytes 196
  3.3 62.6 %copy-start.1 = (bf16[1,2,1024,128]{3,2,1,0:T(8,128)(2,1)S(1)}, bf16[1,2,1024,128]{3,2,1,0:T(8,128)(2,1)}, u32[]{:S(2)}) copy-start(bf16[1,2,1024,128]{3,2,1,0:T(8,128)(2,1)} %grad_ref.1) | copy-start | bytes 1572868
  3.3 62.6 %copy-start.2 = (s32[1,2]{1,0:T(1,128)S(1)}, s32[1,2]{1,0:T(1,128)}, u32[]{:S(2)}) copy-start(s32[1,2]{1,0:T(1,128)} %pads_ref.1) | copy-start | bytes 28
  3.3 62.6 %copy-start.3 = (f32[1,2]{1,0:T(1,128)S(1)}, f32[1,2]{1,0:T(1,128)}, u32[]{:S(2)}) copy-start(f32[1,2]{1,0:T(1,128)} %offset_ref.1) | copy-start | bytes 28
  3.3 39.4 %all-to-all-start = ((bf16[16,104,128]{2,1,0:T(8,128)(2,1)}), bf16[16,104,128]{2,1,0:T(8,128)(2,1)S(1)}, u32[]{:S(2)}, u32[]{:S(2)}) async-start(bf16[16,104,128]{2,1,0:T(8,128)(2,1)} %shard_map.145), calls=%async_computation | async-start | bytes 851968 | tf_op jit(solution)/shard_map/all_to_all | solution.py:454
